TPU v7x, 32 devices: a whole 2x2x4 slice. The times are simulated.
32 devices in a mesh: groups: 2 (over x), mp: 8 (over z, y), rows: 2 (over core).
Axes of the slice: x: 2, y: 2, z: 4, core: 2. Of those that a mesh axis runs over, the one named last changes fastest.
Arguments:
- layer_input: bfloat16 [1536, 5120], P(('groups', 'rows')), parts along dimension 0, may hold values from -6 to 6
- norm_gain: float32 [5120], replicated, may hold values from 0.5 to 1.5
- norm_bias: float32 [5120], replicated, may hold values from -1.5 to 1.5
- w_query_key: bfloat16 [2, 5120, 4096], P(None, None, 'mp'), may hold values from -1 to 1
- w_value: bfloat16 [5120, 4096], P(None, 'mp'), may hold values from -0.078125 to 0.078125
- w_out: bfloat16 [4096, 5120], P('mp'), may hold values from -0.75 to 0.75
- w_maps: bfloat16 [32, 128], replicated, may hold values from -1 to 1
- b_maps: float32 [128], replicated, may hold values from -3 to 3
- pair_gain: float32 [128], replicated, may hold values from 0.5 to 1.5
- pair_bias: float32 [128], replicated, may hold values from -3 to 3
- w_up: bfloat16 [128, 512], replicated, may hold values from -0.5 to 0.5
- b_up: float32 [512], replicated, may hold values from -3 to 3
- w_down: bfloat16 [512, 128], replicated, may hold values from -0.25 to 0.25
- b_down: float32 [128], replicated, may hold values from -3 to 3
Outputs:
- attention: float32 [1536, 5120], P(('groups', 'rows'), 'mp'), parts along dimension 0
- pair_features: bfloat16 [1536, 768, 128], P(('groups', 'rows'), 'mp'), parts along dimension 0
There are 2 independent parts, one for each index of `groups`. A program takes and returns all parts, laid end to end along the dimension named above; an argument that names none is the same for every part. Nothing has to cross between parts.
All inputs are finite; a program needn't handle non-finite values.
Results may differ from a plain program's by a relative error of at most 0.0055.
The roundings to bfloat16 on the way count: a program that leaves them out, or rounds other values in their place, can miss the bound.
Values may be sent and summed in bfloat16 or wider, within the bound.
No kernel may reach another device: no remote copies, remote signals or barrier semaphores. Data moves between devices by JAX's collectives and lax.ppermute only.
A program may use at most 192 MiB of HBM per device.

v0:
```python
import math

import jax
import jax.numpy as jnp
from jax import lax
from jax.sharding import PartitionSpec as P

HD = 128


def layer_norm(values, gain, bias):
    average = jnp.mean(values, axis=-1, keepdims=True)
    centered = values - average
    variance = jnp.mean(centered * centered, axis=-1, keepdims=True)
    return centered * lax.rsqrt(variance + 1e-05) * gain + bias


def rotate(values, positions):
    half = values.shape[-1] // 2
    freqs = 10000.0 ** (-jnp.arange(half, dtype=jnp.float32) / half)
    angles = positions.astype(jnp.float32)[:, None] * freqs[None, :]
    cosine = jnp.cos(angles)[:, None, :]
    sine = jnp.sin(angles)[:, None, :]
    lower = values[..., :half]
    upper = values[..., half:]
    return jnp.concatenate([lower * cosine - upper * sine, upper * cosine + lower * sine], axis=-1)


def project_rotated(normed, weight, positions):
    count = normed.shape[0]
    projected = jnp.dot(normed, weight, preferred_element_type=jnp.float32)
    projected = projected.reshape(count, weight.shape[1] // HD, HD)
    return rotate(projected, positions).astype(jnp.bfloat16).reshape(count, weight.shape[1])


def pair_block(maps, w_maps, b_maps, pair_gain, pair_bias, w_up, b_up, w_down, b_down, factor):
    mixed = (
        jnp.einsum("hrc,hp->rcp", maps, w_maps, preferred_element_type=jnp.float32) * factor
        + b_maps
    )
    normed = layer_norm(mixed, pair_gain, pair_bias).astype(jnp.bfloat16)
    hidden = jax.nn.relu(
        jnp.einsum("rcp,pt->rct", normed, w_up, preferred_element_type=jnp.float32) + b_up
    ).astype(jnp.bfloat16)
    return (
        jnp.einsum("rct,tp->rcp", hidden, w_down, preferred_element_type=jnp.float32) + b_down
    ).astype(jnp.bfloat16)


def per_device(
    layer_input,
    norm_gain,
    norm_bias,
    w_query_key,
    w_value,
    w_out,
    w_maps,
    b_maps,
    pair_gain,
    pair_bias,
    w_up,
    b_up,
    w_down,
    b_down,
):
    tok_rows = layer_input.shape[0]
    tokens_all = tok_rows * lax.axis_size("rows")
    local_heads = w_value.shape[1] // HD
    normed = layer_norm(layer_input.astype(jnp.float32), norm_gain, norm_bias).astype(jnp.bfloat16)
    own_positions = lax.axis_index("rows") * tok_rows + jnp.arange(tok_rows, dtype=jnp.int32)
    queries = project_rotated(normed, w_query_key[0], own_positions)
    keys_local = project_rotated(normed, w_query_key[1], own_positions)
    values_local = jnp.dot(normed, w_value, preferred_element_type=jnp.float32).astype(jnp.bfloat16)
    keys_all, values_all = (
        lax.all_gather(keys_local, "rows", axis=0, tiled=True),
        lax.all_gather(values_local, "rows", axis=0, tiled=True),
    )
    head_queries = queries.reshape(tok_rows, local_heads, HD)
    head_keys = keys_all.reshape(tokens_all, local_heads, HD)
    head_values = values_all.reshape(tokens_all, local_heads, HD)
    scores = jnp.einsum(
        "qhd,khd->hqk", head_queries, head_keys, preferred_element_type=jnp.float32
    ) / math.sqrt(HD)
    maps = jax.nn.softmax(scores, axis=-1).astype(jnp.bfloat16)
    context = jnp.einsum("hqk,khd->qhd", maps, head_values, preferred_element_type=jnp.float32)
    context = context.astype(jnp.bfloat16).reshape(tok_rows, local_heads * HD)
    partial_sums = jnp.dot(context, w_out, preferred_element_type=jnp.float32)
    attention = lax.psum_scatter(partial_sums, "mp", scatter_dimension=1, tiled=True)
    factor = float(tokens_all)
    pair_features = pair_block(
        lax.all_to_all(maps, "mp", split_axis=2, concat_axis=0, tiled=True),
        w_maps,
        b_maps,
        pair_gain,
        pair_bias,
        w_up,
        b_up,
        w_down,
        b_down,
        factor,
    )
    return (attention, pair_features)


def solution(mesh):
    in_specs = (
        P(("groups", "rows"), None),
        P(),
        P(),
        P(None, None, "mp"),
        P(None, "mp"),
        P("mp", None),
        P(),
        P(),
        P(),
        P(),
        P(),
        P(),
        P(),
        P(),
    )
    out_specs = (P(("groups", "rows"), "mp"), P(("groups", "rows"), "mp", None))
    return jax.shard_map(
        per_device, mesh=mesh, in_specs=in_specs, out_specs=out_specs, check_vma=False
    )
```

profile of v0, /device:TPU:0, one launch (start us, length us, event | category | flops | bytes accessed | tf_op | source)
XLA Modules:
  0.0 278.5 jit_solution(13034507859399231984)
XLA Ops:
  7.2 0.0 copy-start
  7.2 0.0 copy-start.5
  7.2 0.0 copy-start.6
  7.2 0.0 reduce-scatter.2.cloned.1.call-start
  7.3 0.0 copy-start.1
  7.3 2.9 %convert_reduce_fusion = f32[384]{0:T(512)S(1)} fusion(bf16[384,5120]{1,0:T(8,128)(2,1)} %param.14), kind=kLoop, calls=%fused_computation.12 | loop fusion | flops 3931776 | bytes 3933696 | tf_op jit(solution)/shard_map/reduce_sum | solution.py:12
  10.2 3.3 %fusion.21 = f32[384]{0:T(512)S(1)} fusion(bf16[384,5120]{1,0:T(8,128)(2,1)} %param.14, f32[384]{0:T(512)S(1)} %broadcast_multiply_fusion.1), kind=kLoop, calls=%fused_computation.21 | loop fusion | flops 7863936 | bytes 3935232 | tf_op jit(solution)/shard_map/reduce_sum | solution.py:14
  13.5 0.0 copy-done.5
  13.5 0.0 copy-done.6
  13.5 0.0 copy-done.1
  13.5 4.7 %convolution_convert_fusion.1 = bf16[384,512]{1,0:T(8,128)(2,1)S(1)} fusion(bf16[5120,512]{1,0:T(8,128)(2,1)} %param.18, bf16[384,5120]{1,0:T(8,128)(2,1)S(1)} %copy-done.1, f32[5120]{0:T(1024)S(1)} %copy-done.5, f32[5120]{0:T(1024)S(1)} %copy-done.6, f32[384]{0:T(512)S(1)} %add_rsqrt_fusion.1, f32[384]{0:T(512)S(1)} %broadcast_multiply_fusion.1), kind=kOutput, calls=%fused_computation.37 | convolution fusion | flops 2025259008 | bytes 9612288 | tf_op jit(solution)/shard_map/dot_general | solution.py:73
  18.2 2.8 %all_gather.6 = bf16[768,512]{1,0:T(8,128)(2,1)S(1)} all-gather(bf16[384,512]{1,0:T(8,128)(2,1)S(1)} %convolution_convert_fusion.1), channel_id=1, replica_groups=mesh['groups'=2,'mp'=8,'rows'=2] {'rows'}, dimensions={0}, use_global_device_ids=true | all-gather | bytes 1179648 | tf_op jit(solution)/shard_map/all_gather | solution.py:76
  21.1 0.3 copy.43
  21.3 8.8 %slice_bitcast_fusion.1 = (bf16[512,5120]{0,1:T(8,128)(2,1)}, bf16[512,5120]{0,1:T(8,128)(2,1)}) fusion(bf16[2,5120,512]{2,1,0:T(8,128)(2,1)} %param.17), kind=kLoop, calls=%fused_computation.26 | loop fusion | bytes 20971520 | tf_op jit(solution)/shard_map/dot_general | solution.py:31
  30.1 8.0 %copy.30 = bf16[512,5120]{1,0:T(8,128)(2,1)} copy(bf16[512,5120]{0,1:T(8,128)(2,1)} %get-tuple-element.8) | data formatting | bytes 10485760 | tf_op jit(solution)/shard_map/dot_general | solution.py:31
  38.1 6.7 %fusion.28 = f32[384,4,128]{0,2,1:T(8,128)S(1)} fusion(bf16[4,128,5120]{2,1,0:T(8,128)(2,1)} %bitcast.52, bf16[384,5120]{1,0:T(8,128)(2,1)} %param.14, f32[5120]{0:T(1024)S(1)} %copy-done.5, f32[5120]{0:T(1024)S(1)} %copy-done.6, f32[384]{0:T(512)S(1)} %add_rsqrt_fusion.1, f32[384]{0:T(512)S(1)} %broadcast_multiply_fusion.1), kind=kOutput, calls=%fused_computation.33 | convolution fusion | flops 2025062400 | bytes 10005504 | tf_op jit(solution)/shard_map/dot_general | solution.py:31
  44.8 7.9 %copy.31 = bf16[512,5120]{1,0:T(8,128)(2,1)} copy(bf16[512,5120]{0,1:T(8,128)(2,1)} %get-tuple-element.9) | data formatting | bytes 10485760 | tf_op jit(solution)/shard_map/dot_general | solution.py:31
  52.7 6.7 %fusion.26 = f32[384,4,128]{0,2,1:T(8,128)S(1)} fusion(bf16[4,128,5120]{2,1,0:T(8,128)(2,1)} %bitcast.51, bf16[384,5120]{1,0:T(8,128)(2,1)} %param.14, f32[5120]{0:T(1024)S(1)} %copy-done.5, f32[5120]{0:T(1024)S(1)} %copy-done.6, f32[384]{0:T(512)S(1)} %add_rsqrt_fusion.1, f32[384]{0:T(512)S(1)} %broadcast_multiply_fusion.1), kind=kOutput, calls=%fused_computation.31 | convolution fusion | flops 2025062400 | bytes 10005504 | tf_op jit(solution)/shard_map/dot_general | solution.py:31
  59.4 0.4 multiply_cosine_fusion
  59.9 0.2 subtract_convert_fusion.1
  60.1 3.0 %all_gather.7 = bf16[768,512]{0,1:T(8,128)(2,1)S(1)} all-gather(bf16[384,512]{0,1:T(8,128)(2,1)S(1)} %bitcast.55), channel_id=1, replica_groups=mesh['groups'=2,'mp'=8,'rows'=2] {'rows'}, dimensions={0}, use_global_device_ids=true | all-gather | bytes 1179648 | tf_op jit(solution)/shard_map/all_gather | solution.py:75
  63.1 3.8 %fusion.52 = (f32[4,384]{1,0:T(4,128)S(1)}, f32[4,384,768]{2,1,0:T(8,128)}) fusion(bf16[768,4,128]{0,2,1:T(8,128)(2,1)S(1)} %bitcast.56, bf16[384,4,64]{0,2,1:T(8,128)(2,1)S(1)} %get-tuple-element.11, bf16[384,4,64]{0,2,1:T(8,128)(2,1)S(1)} %get-tuple-element.10), kind=kOutput, calls=%fused_computation.63 | convolution fusion | flops 306316032 | bytes 5904384 | tf_op jit(solution)/shard_map/sub | solution.py:84
  66.9 2.8 %divide_convert_fusion = bf16[4,384,768]{2,1,0:T(8,128)(2,1)S(1)} fusion(f32[4,384,768]{2,1,0:T(8,128)} %get-tuple-element.19, f32[4,384]{1,0:T(4,128)S(1)} %get-tuple-element.18), kind=kLoop, calls=%fused_computation.27 | loop fusion | flops 2359296 | bytes 7084032 | tf_op jit(solution)/shard_map/convert_element_type | solution.py:84
  69.8 0.8 convolution_convert_fusion
  70.5 0.0 slice-done
  70.6 0.3 slice-done.1
  70.8 5.4 %fusion.53 = f32[384,5120]{1,0:T(8,128)} fusion(bf16[384,512]{0,1:T(8,128)(2,1)S(1)} %bitcast.54, bf16[512,5120]{1,0:T(8,128)(2,1)S(1)} %bitcast.50), kind=kOutput, calls=%fused_computation.64 | convolution fusion | flops 2013265920 | bytes 13500416 | tf_op jit(solution)/shard_map/dot_general | solution.py:87
  76.3 0.0 reduce-scatter.2.cloned.1.call-update
  76.3 3.4 %copy.35 = bf16[4,384,768]{1,0,2:T(4,128)(2,1)} copy(bf16[4,384,768]{2,1,0:T(8,128)(2,1)S(1)} %divide_convert_fusion) | data formatting | bytes 4718592 | tf_op jit(solution)/shard_map/convert_element_type | solution.py:84
  79.6 116.8 %all_to_all.18 = bf16[4,384,768]{1,0,2:T(4,128)(2,1)S(1)} all-to-all(bf16[4,384,768]{1,0,2:T(4,128)(2,1)} %copy.35), channel_id=1, replica_groups=mesh['groups'=2,'mp'=8,'rows'=2] {'mp'}, dimensions={2} | all-to-all | bytes 4718592 | tf_op jit(solution)/shard_map/all_to_all | solution.py:91
  196.4 0.3 copy.36
  196.7 3.2 %copy.37 = bf16[8,4,384,96]{2,1,0,3:T(4,128)(2,1)} copy(bf16[8,4,384,96]{2,3,0,1:T(8,128)(2,1)S(1)} %bitcast.48) | data formatting | bytes 4718592 | tf_op jit(solution)/shard_map/all_to_all | solution.py:91
  200.0 3.9 %all_to_all.16 = bf16[32,384,96]{1,0,2:T(8,128)(2,1)S(1)} reshape(bf16[8,4,384,96]{2,1,0,3:T(4,128)(2,1)} %copy.37) | data formatting | bytes 4718592 | tf_op jit(solution)/shard_map/all_to_all | solution.py:91
  203.9 0.0 copy-done.2
  203.9 0.0 copy-done.3
  203.9 7.9 %fusion.6 = (f32[384,96]{0,1:T(8,128)S(1)}, f32[384,96,128]{0,2,1:T(8,128)}) fusion(f32[128]{0:T(128)S(1)} %copy-done.3, bf16[32,384,96]{1,0,2:T(8,128)(2,1)S(1)} %all_to_all.16, bf16[32,128]{1,0:T(8,128)(2,1)S(1)} %copy-done.2), kind=kOutput, calls=%fused_computation.10 | convolution fusion | flops 316108800 | bytes 21389824 | tf_op jit(solution)/shard_map/hrc,hp->rcp/dot_general | solution.py:38
  211.8 0.0 copy-start.4
  211.9 0.0 copy-start.7
  211.9 0.0 copy-start.8
  211.9 0.0 copy-start.9
  211.9 0.0 copy-start.10
  211.9 11.8 %multiply_reduce_fusion = f32[384,96]{0,1:T(8,128)S(1)} fusion(f32[384,96,128]{0,2,1:T(8,128)} %get-tuple-element.21, f32[384,96]{0,1:T(8,128)S(1)} %broadcast_multiply_fusion, f32[128]{0:T(128)S(1)} %copy-done.3), kind=kLoop, calls=%fused_computation.8 | loop fusion | flops 23556096 | bytes 19169792 | tf_op jit(solution)/shard_map/reduce_sum | solution.py:14
  223.8 0.0 copy-done
  223.8 0.0 copy-done.4
  223.8 0.0 copy-done.7
  223.8 26.5 %add_convert_fusion = bf16[384,96,128]{2,0,1:T(8,128)(2,1)} fusion(f32[128]{0:T(128)S(1)} %copy-done.8, f32[512]{0:T(512)S(1)} %copy-done.7, f32[384,96,128]{0,2,1:T(8,128)} %get-tuple-element.21, f32[128]{0:T(128)S(1)} %copy-done.9, f32[128]{0:T(128)S(1)} %copy-done.10, f32[384,96]{0,1:T(8,128)S(1)} %add_rsqrt_fusion, ...), kind=kOutput, calls=%fused_computation.6 | convolution fusion | flops 9762766848 | bytes 28872704 | tf_op jit(solution)/shard_map/rct,tp->rcp/dot_general | solution.py:46
  250.4 13.6 %copy.39 = bf16[384,96,128]{2,1,0:T(8,128)(2,1)} copy(bf16[384,96,128]{2,0,1:T(8,128)(2,1)} %add_convert_fusion) | data formatting | bytes 18874368
  264.0 7.4 %reduce-scatter.2.cloned.1.call-done = f32[384,640]{1,0:T(8,128)} async-done(((f32[384,5120]{1,0:T(8,128)}), f32[384,640]{1,0:T(8,128)}) %reduce-scatter.2.cloned.1.call-update) | async-done | bytes 983056 | tf_op jit(solution)/shard_map/reduce_scatter | solution.py:88
  (15 shorter events, 0.1 us)
Async XLA Ops:
  7.2 216.6 %copy-start = (bf16[512,128]{1,0:T(8,128)(2,1)S(1)}, bf16[512,128]{1,0:T(8,128)(2,1)}, u32[]{:S(2)}) copy-start(bf16[512,128]{1,0:T(8,128)(2,1)} %param.26) | copy-start | bytes 393220
  7.2 6.3 %copy-start.5 = (f32[5120]{0:T(1024)S(1)}, f32[5120]{0:T(1024)}, u32[]{:S(2)}) copy-start(f32[5120]{0:T(1024)} %param.16) | copy-start | bytes 61444
  7.2 6.3 %copy-start.6 = (f32[5120]{0:T(1024)S(1)}, f32[5120]{0:T(1024)}, u32[]{:S(2)}) copy-start(f32[5120]{0:T(1024)} %param.15) | copy-start | bytes 61444
  7.2 264.2 %reduce-scatter.2.cloned.1.call-start = ((), (), s32[]{:S(2)}) async-start(), calls=%async_computation.2 | async-start | bytes 8847360 | tf_op jit(solution)/shard_map/reduce_scatter | solution.py:88
  7.3 6.2 %copy-start.1 = (bf16[384,5120]{1,0:T(8,128)(2,1)S(1)}, bf16[384,5120]{1,0:T(8,128)(2,1)}, u32[]{:S(2)}) copy-start(bf16[384,5120]{1,0:T(8,128)(2,1)} %param.14) | copy-start | bytes 11796484
  66.9 3.6 %slice-start = ((s8[5242880]{0:T(1024)(128)(4,1)}), s8[4194304]{0:T(1024)(128)(4,1)S(1)}, s32[]{:S(2)}) async-start(s8[5242880]{0:T(1024)(128)(4,1)} %bitcast.49), calls=%async_computation.3 | async-start | bytes 8388608
  66.9 3.9 %slice-start.1 = ((s8[5242880]{0:T(1024)(128)(4,1)}), s8[1048576]{0:T(1024)(128)(4,1)S(1)}, s32[]{:S(2)}) async-start(s8[5242880]{0:T(1024)(128)(4,1)} %bitcast.49), calls=%async_computation.4 | async-start | bytes 2097152
  196.4 7.5 %copy-start.2 = (bf16[32,128]{1,0:T(8,128)(2,1)S(1)}, bf16[32,128]{1,0:T(8,128)(2,1)}, u32[]{:S(2)}) copy-start(bf16[32,128]{1,0:T(8,128)(2,1)} %param.20) | copy-start | bytes 24580
  196.4 7.5 %copy-start.3 = (f32[128]{0:T(128)S(1)}, f32[128]{0:T(128)}, u32[]{:S(2)}) copy-start(f32[128]{0:T(128)} %param.21) | copy-start | bytes 1540
  211.8 11.9 %copy-start.4 = (bf16[128,512]{1,0:T(8,128)(2,1)S(1)}, bf16[128,512]{1,0:T(8,128)(2,1)}, u32[]{:S(2)}) copy-start(bf16[128,512]{1,0:T(8,128)(2,1)} %param.24) | copy-start | bytes 393220
  211.9 11.9 %copy-start.7 = (f32[512]{0:T(512)S(1)}, f32[512]{0:T(512)}, u32[]{:S(2)}) copy-start(f32[512]{0:T(512)} %param.25) | copy-start | bytes 6148
  211.9 11.9 %copy-start.8 = (f32[128]{0:T(128)S(1)}, f32[128]{0:T(128)}, u32[]{:S(2)}) copy-start(f32[128]{0:T(128)} %param.27) | copy-start | bytes 1540
  211.9 11.9 %copy-start.9 = (f32[128]{0:T(128)S(1)}, f32[128]{0:T(128)}, u32[]{:S(2)}) copy-start(f32[128]{0:T(128)} %param.23) | copy-start | bytes 1540
  211.9 11.9 %copy-start.10 = (f32[128]{0:T(128)S(1)}, f32[128]{0:T(128)}, u32[]{:S(2)}) copy-start(f32[128]{0:T(128)} %param.22) | copy-start | bytes 1540
Sparse Core Ops, SparseCore 0:
  76.4 194.9 reduce-scatter.1
where the time goes:
time: 283 us; the launch traced here: 279 us
  blocking collectives  123 us (43%)
  matrix products  62.7 us (22%)
  local copies, waits for them, and re-layouts  49.7 us (18%)
  other arithmetic  21.6 us (8%)
  between operations  14.6 us (5%)
  waiting for transfers between devices  7.43 us (3%)
    all_to_all x1, blocking collectives, per_device(): lax.all_to_all(maps, 'mp', split_axis=2, concat_axis=0, tiled=True)  117 us
    dot_general x1, matrix products, pair_block(): jnp.einsum('rct,tp->rcp', hidden, w_down, preferred_element_type=jnp.floa...  26.5 us
    dot_general x3, local copies, waits for them, and re-layouts, project_rotated(): projected = jnp.dot(normed, weight, preferred_element_type=jnp.float32)  24.7 us
    reduce_sum x2, other arithmetic, layer_norm(): variance = jnp.mean(centered * centered, axis=-1, keepdims=True)  15.1 us
    unnamed x27, local copies, waits for them, and re-layouts  13.9 us
    dot_general x2, matrix products, project_rotated(): projected = jnp.dot(normed, weight, preferred_element_type=jnp.float32)  13.4 us
    dot_general x1, matrix products, pair_block(): jnp.einsum('hrc,hp->rcp', maps, w_maps, preferred_element_type=jnp.float32)  7.93 us
    all_to_all x3, local copies, waits for them, and re-layouts, per_device(): lax.all_to_all(maps, 'mp', split_axis=2, concat_axis=0, tiled=True)  7.44 us
  transfers between devices with their start and end apart: 1, of which 1 were waited for; matrix products, arithmetic and copies ran while one was open for 24% of the time, Pallas kernels for 0%

commit v1 on v0

--- a/solution.py
+++ b/solution.py
@@ -1,11 +1,619 @@
+import functools
 import math
 
 import jax
 import jax.numpy as jnp
 from jax import lax
+from jax.experimental import pallas as pl
+from jax.experimental.pallas import tpu as pltpu
 from jax.sharding import PartitionSpec as P
 
+
 HD = 128
+F32 = jnp.float32
+BF16 = jnp.bfloat16
+ROOT = math.sqrt(HD)
+
+
+def params(*axes, mib=24):
+    return pltpu.CompilerParams(
+        dimension_semantics=axes if axes else None, vmem_limit_bytes=mib * 1024 * 1024
+    )
+
+
+def cost(flops, moved, transcendentals=0):
+    return pl.CostEstimate(
+        flops=int(flops), bytes_accessed=int(moved), transcendentals=int(transcendentals)
+    )
+
+
+def sds(shape, dtype):
+    return jax.ShapeDtypeStruct(shape, dtype)
+
+
+VMEM = pl.BlockSpec(memory_space=pltpu.VMEM)
+ANYWHERE = pl.BlockSpec(memory_space=pl.ANY)
+HBM = pl.BlockSpec(memory_space=pltpu.HBM)
+SMEM = pl.BlockSpec(memory_space=pltpu.SMEM)
+
+
+def turn(block, cosine, sine):
+    pieces = []
+    for head in range(block.shape[1] // HD):
+        one = block[:, head * HD : (head + 1) * HD]
+        pieces.append(one * cosine + pltpu.roll(one, HD // 2, 1) * sine)
+    return jnp.concatenate(pieces, axis=1)
+
+
+def project_kernel(
+    x_ref, gain_ref, bias_ref, wqk_ref, wv_ref, cos_ref, sin_ref, q_ref, kv_ref, x, normed, w, x_sems, w_sems
+):
+    rows, width = x.shape
+    columns = q_ref.shape[1]
+    step, chunks, tile = 16, x_sems.shape[0], min(256, columns)
+    parts = w_sems.shape[1]
+    deep = width // parts
+    piece = rows // chunks
+    x_copies = [
+        pltpu.make_async_copy(
+            x_ref.at[n * piece : (n + 1) * piece], x.at[n * piece : (n + 1) * piece], x_sems.at[n]
+        )
+        for n in range(chunks)
+    ]
+    sources = (wqk_ref.at[1], wqk_ref.at[0], wv_ref)
+    w_copies = [
+        pltpu.make_async_copy(
+            source.at[n * deep : (n + 1) * deep],
+            w.at[which, n * deep : (n + 1) * deep],
+            w_sems.at[which, n],
+        )
+        for which, source in enumerate(sources)
+        for n in range(parts)
+    ]
+    for copy in x_copies + w_copies:
+        copy.start()
+
+    def body(i, carry):
+        at = pl.ds(pl.multiple_of(i * step, step), step)
+
+        def lanes(n):
+            return slice(n * HD, (n + 1) * HD)
+
+        def total(one):
+            parts = [jnp.zeros((step, HD), F32) for _ in range(4)]
+            for n in range(width // HD):
+                parts[n % 4] = parts[n % 4] + one(x[at, lanes(n)].astype(F32))
+            whole = (parts[0] + parts[1]) + (parts[2] + parts[3])
+            return jnp.sum(whole, axis=1, keepdims=True) * (1.0 / width)
+
+        mean = total(lambda v: v)
+        variance = total(lambda v: (v - mean) * (v - mean))
+        scale = lax.rsqrt(variance + 1e-05)
+        for n in range(width // HD):
+            scaled = (x[at, lanes(n)].astype(F32) - mean) * scale
+            normed[at, lanes(n)] = (scaled * gain_ref[:, lanes(n)] + bias_ref[:, lanes(n)]).astype(BF16)
+        return carry
+
+    for n in range(chunks):
+        x_copies[n].wait()
+        lax.fori_loop(n * piece // step, (n + 1) * piece // step, body, 0, unroll=2)
+    cosine = jnp.concatenate([cos_ref[...], cos_ref[...]], axis=1)
+    sine = jnp.concatenate([-sin_ref[...], sin_ref[...]], axis=1)
+    for which in range(3):
+        for n in range(parts):
+            w_copies[which * parts + n].wait()
+        for n in range(columns // tile):
+            block = jnp.dot(
+                normed[...], w[which, :, n * tile : (n + 1) * tile], preferred_element_type=F32
+            )
+            if which < 2:
+                block = turn(block, cosine, sine)
+            at = n * tile
+            if which == 0:
+                kv_ref[:, at : at + tile] = block.astype(BF16)
+            elif which == 1:
+                q_ref[:, at : at + tile] = block.astype(BF16)
+            else:
+                kv_ref[:, columns + at : columns + at + tile] = block.astype(BF16)
+
+
+def project(x, gain, bias, w_query_key, w_value, cosine, sine):
+    rows, width = x.shape
+    columns = w_value.shape[1]
+    return pl.pallas_call(
+        project_kernel,
+        in_specs=[HBM, VMEM, VMEM, HBM, HBM, VMEM, VMEM],
+        out_specs=[VMEM, VMEM],
+        out_shape=[sds((rows, columns), BF16), sds((rows, 2 * columns), BF16)],
+        scratch_shapes=[
+            pltpu.VMEM((rows, width), BF16),
+            pltpu.VMEM((rows, width), BF16),
+            pltpu.VMEM((3, width, columns), BF16),
+            pltpu.SemaphoreType.DMA((4,)),
+            pltpu.SemaphoreType.DMA((3, 2)),
+        ],
+        compiler_params=params(mib=44),
+        cost_estimate=cost(6 * rows * width * columns, 2 * width * (rows + 3 * columns)),
+        name="project",
+    )(x, gain.reshape(1, width), bias.reshape(1, width), w_query_key, w_value, cosine, sine)
+
+
+def attend_kernel(
+    ring, at_ref, q_ref, own_ref, there_ref, context_ref, local_ref, *rest
+):
+    share_refs, level_ref = rest[:-1], rest[-1]
+    rows, width = q_ref.shape
+    heads = width // HD
+    columns = local_ref.shape[0] // 2 - 8
+    core, z, y = at_ref[0], at_ref[1], at_ref[2]
+    lane = lax.broadcasted_iota(jnp.int32, (rows, HD), 1)
+    table = jnp.zeros((rows, HD), F32)
+    contract = (((1,), (1,)), ((), ()))
+    for head in range(heads):
+        at = slice(head * HD, (head + 1) * HD)
+        at_v = slice(width + head * HD, width + (head + 1) * HD)
+        scores = [
+            lax.dot_general(q_ref[:, at], ref[:, at], contract, preferred_element_type=F32)
+            * (1.0 / ROOT)
+            for ref in (own_ref, there_ref)
+        ]
+        top = jnp.max(jnp.maximum(scores[0], scores[1]), axis=1, keepdims=True)
+        raised = [jnp.exp(part - top) for part in scores]
+        total = jnp.sum(raised[0] + raised[1], axis=1, keepdims=True)
+        inverse = 1.0 / total
+        maps = [(part * inverse).astype(BF16) for part in raised]
+        context_ref[:, at] = (
+            jnp.dot(maps[0], own_ref[:, at_v], preferred_element_type=F32)
+            + jnp.dot(maps[1], there_ref[:, at_v], preferred_element_type=F32)
+        ).astype(BF16)
+        level = (top + jnp.log(total)) * ROOT
+        high = level.astype(BF16).astype(F32)
+        middle = (level - high).astype(BF16).astype(F32)
+        low = (level - high - middle).astype(BF16).astype(F32)
+        for piece, part in enumerate((high, middle, low)):
+            table = jnp.where(lane == 3 * head + piece, part, table)
+    level_ref[...] = jnp.zeros_like(level_ref)
+    level_ref[:, 0:rows] = table.T[0:16].astype(BF16)
+
+    def key_rows(chip, which):
+        token = chip * (2 * columns) + which * columns
+        holder = (token >= rows).astype(jnp.int32)
+        start = pl.ds(pl.multiple_of(token - holder * rows, 32), columns)
+        mine = (holder == core).astype(F32)
+        near = own_ref[start, 0:width].astype(F32)
+        far = there_ref[start, 0:width].astype(F32)
+        return (near * mine + far * (1.0 - mine)).astype(BF16)
+
+    local_ref[0:columns, :] = key_rows(z, y)
+    local_ref[columns : 2 * columns, :] = key_rows(z, 1 - y)
+    local_ref[2 * columns : 2 * columns + 16, :] = level_ref[...]
+    for distance, share_ref in enumerate(share_refs, 1):
+        chip = lax.rem(z + distance, ring)
+        share_ref[0:columns, :] = key_rows(chip, core)
+        share_ref[columns : columns + 16, :] = level_ref[...]
+
+
+def attend(at, queries, own, there, ring, columns):
+    rows, width = queries.shape
+    tokens = 2 * rows
+    return pl.pallas_call(
+        functools.partial(attend_kernel, ring),
+        in_specs=[SMEM, VMEM, VMEM, VMEM],
+        out_specs=[VMEM] * (ring + 1),
+        out_shape=[sds((rows, width), BF16), sds((2 * columns + 16, width), BF16)]
+        + [sds((columns + 16, width), BF16)] * (ring - 1),
+        scratch_shapes=[pltpu.VMEM((16, width), BF16)],
+        compiler_params=params(),
+        cost_estimate=cost(4 * rows * tokens * width, 8 * rows * width, rows * tokens * width // HD),
+        name="attend",
+    )(at, queries, own, there)
+
+
+def pack_kernel(count, at_ref, w_ref, out_ref, sems):
+    depth, wide = out_ref.shape
+    tile = wide // count
+    core, z, y = at_ref[0], at_ref[1], at_ref[2]
+    copies = []
+    for n in range(count):
+        block = 2 * lax.rem(z + (2 * count - 1 - n), count) + 1 - y
+        copies.append(
+            pltpu.make_async_copy(
+                w_ref.at[
+                    pl.ds(pl.multiple_of(core * depth, depth), depth),
+                    pl.ds(pl.multiple_of(block * tile, tile), tile),
+                ],
+                out_ref.at[:, n * tile : (n + 1) * tile],
+                sems.at[n],
+            )
+        )
+    for copy in copies:
+        copy.start()
+    for copy in copies:
+        copy.wait()
+
+
+def pack_columns(at, w, count):
+    depth, wide = w.shape[0] // 2, w.shape[1] // 2
+    return pl.pallas_call(
+        functools.partial(pack_kernel, count),
+        in_specs=[SMEM, HBM],
+        out_specs=VMEM,
+        out_shape=sds((depth, wide), BF16),
+        scratch_shapes=[pltpu.SemaphoreType.DMA((count,))],
+        compiler_params=params(),
+        cost_estimate=cost(0, 4 * depth * wide),
+        name="pack_columns",
+    )(at, w)
+
+
+def project_out_kernel(at_ref, near_ref, far_ref, w_ref, w_same_ref, w_cross_ref, *rest):
+    out_refs, (w, sems) = rest[:-2], rest[-2:]
+    count = len(out_refs)
+    tile = out_refs[0].shape[1]
+    half = w_same_ref.shape[0]
+    core, z, y = at_ref[0], at_ref[1], at_ref[2]
+    copies = []
+    for n in range(count):
+        block = 2 * lax.rem(z + (2 * count - 1 - n), count) + y
+        copies.append(
+            pltpu.make_async_copy(
+                w_ref.at[:, pl.ds(pl.multiple_of(block * tile, tile), tile)], w.at[n], sems.at[n]
+            )
+        )
+    for copy in copies:
+        copy.start()
+    same = far_ref[:, pl.ds(pl.multiple_of(core * half, half), half)]
+    cross = far_ref[:, pl.ds(pl.multiple_of((1 - core) * half, half), half)]
+    for n, out_ref in enumerate(out_refs):
+        lanes = slice(n * tile, (n + 1) * tile)
+        block = jnp.dot(same, w_same_ref[:, lanes], preferred_element_type=F32) + jnp.dot(
+            cross, w_cross_ref[:, lanes], preferred_element_type=F32
+        )
+        copies[n].wait()
+        block = block + jnp.dot(near_ref[...], w[n], preferred_element_type=F32)
+        out_ref[...] = block.astype(out_ref.dtype)
+
+
+def project_out(at, near, far, w, w_same, w_cross, count):
+    rows, depth = near.shape
+    _, wide = w_same.shape
+    tile = wide // count
+    return pl.pallas_call(
+        project_out_kernel,
+        in_specs=[SMEM, VMEM, VMEM, ANYWHERE, VMEM, VMEM],
+        out_specs=[VMEM] * count,
+        out_shape=[sds((rows, tile), BF16)] + [sds((rows, tile), F32)] * (count - 1),
+        scratch_shapes=[
+            pltpu.VMEM((count, depth, tile), BF16),
+            pltpu.SemaphoreType.DMA((count,)),
+        ],
+        compiler_params=params(),
+        cost_estimate=cost(4 * rows * depth * wide, 4 * wide * (rows + depth)),
+        name="project_out",
+    )(at, near, far, w, w_same, w_cross)
+
+
+def pair_maps_kernel(sources, at_ref, *refs):
+    own_ref, other_ref = refs[-2:]
+    rows = own_ref.shape[1]
+    width = refs[0].shape[1]
+    heads = width // HD
+    wide = own_ref.shape[2]
+    columns = wide // heads
+    lane_head = lax.broadcasted_iota(jnp.int32, (columns, width), 1) // HD
+    row = lax.broadcasted_iota(jnp.int32, (16, wide), 0)
+    column = lax.broadcasted_iota(jnp.int32, (16, wide), 1)
+    hit = jnp.zeros((16, wide), jnp.bool_)
+    for head in range(heads):
+        inside = (column >= head * columns) & (column < (head + 1) * columns)
+        hit = hit | (inside & (row >= 3 * head) & (row < 3 * head + 3))
+    pick = jnp.where(hit, -1.0, 0.0).astype(BF16)
+    straight = (at_ref[2] == at_ref[0]).astype(F32)
+    taken = 0
+    for place, count in enumerate(sources):
+        q_ref, keys = refs[taken], refs[taken + 1 : taken + count]
+        taken += count
+        if count == 2:
+            pieces = [keys[0][n * columns : (n + 1) * columns, :].astype(F32) for n in range(2)]
+            levels = keys[0][2 * columns : 2 * columns + 16, 0:rows]
+        else:
+            mine = keys[0][0:columns, :].astype(F32)
+            theirs = keys[1][0:columns, :].astype(F32)
+            pieces = [
+                mine * straight + theirs * (1.0 - straight),
+                theirs * straight + mine * (1.0 - straight),
+            ]
+            levels = keys[0][columns : columns + 16, 0:rows]
+        level = lax.dot_general(
+            levels, pick, (((0,), (0,)), ((), ())), preferred_element_type=F32
+        )
+        for k, out_ref in zip(pieces, (own_ref, other_ref)):
+            spread = jnp.concatenate(
+                [jnp.where(lane_head == head, k, 0.0).astype(BF16) for head in range(heads)], axis=0
+            )
+            scores = lax.dot_general(
+                q_ref[...], spread, (((1,), (1,)), ((), ())), preferred_element_type=F32
+            )
+            out_ref[place] = jnp.exp((scores + level) * (1.0 / ROOT)).astype(BF16)
+
+
+def pair_maps(at, sources, columns):
+    rows, width = sources[0][0].shape
+    wide = (width // HD) * columns
+    count = len(sources)
+    flat = [array for source in sources for array in source]
+    return pl.pallas_call(
+        functools.partial(pair_maps_kernel, [len(source) for source in sources]),
+        in_specs=[SMEM] + [VMEM] * len(flat),
+        out_specs=[VMEM] * 2,
+        out_shape=[sds((count, rows, wide), BF16)] * 2,
+        compiler_params=params(),
+        cost_estimate=cost(
+            4 * count * rows * wide * width, 8 * count * rows * wide, 2 * count * rows * wide
+        ),
+        name="pair_maps",
+    )(at, *flat)
+
+
+def pair_kernel(factor, inputs, count, chained, at_ref, *refs):
+    maps_refs = refs[:inputs]
+    (w_maps_ref, b_maps_ref, gain_ref, bias_ref, w_up_ref, b_up_ref, w_down_ref, b_down_ref) = refs[
+        inputs : inputs + 8
+    ]
+    out_ref, spread_ref, up_ref, shift_ref, rows_ref = refs[inputs + 8 + chained :]
+    block = out_ref.shape[0]
+    columns = out_ref.shape[1]
+    chunk = 8 * columns
+    channels = out_ref.shape[2]
+    heads_all = w_maps_ref.shape[0]
+    heads = heads_all // count
+    group = HD // heads_all
+
+    @pl.when(pl.program_id(0) == 0)
+    def _():
+        row = lax.broadcasted_iota(jnp.int32, (heads_all, heads_all), 0)
+        column = lax.broadcasted_iota(jnp.int32, (heads_all, heads_all), 1)
+        ring = count // 2
+        distance = lax.rem(row // heads, ring)
+        chip = lax.rem(at_ref[1] + ring - distance, ring)
+        side = jnp.where(row // heads >= ring, 1 - at_ref[2], at_ref[2])
+        head = (2 * chip + side) * heads + lax.rem(row, heads)
+        sort = jnp.where(column == head, 1.0, 0.0).astype(BF16)
+        w = jnp.dot(sort, w_maps_ref[...], preferred_element_type=F32)
+        w = (w - jnp.sum(w, axis=1, keepdims=True) * (1.0 / channels)) * factor
+        high = w.astype(BF16)
+        low = (w - high.astype(F32)).astype(BF16)
+        spread_ref[...] = jnp.zeros_like(spread_ref)
+        for i in range(group):
+            at = slice(i * channels, (i + 1) * channels)
+            spread_ref[i * heads_all : (i + 1) * heads_all, at] = high
+            spread_ref[HD + i * heads_all : HD + (i + 1) * heads_all, at] = low
+        b = b_maps_ref[...]
+        b = b - jnp.sum(b, axis=1, keepdims=True) * (1.0 / channels)
+        shift_ref[...] = jnp.concatenate([b] * group, axis=1)
+        up_ref[0:channels, :] = w_up_ref[...]
+        b_up = b_up_ref[...]
+        top = b_up.astype(BF16).astype(F32)
+        middle = (b_up - top).astype(BF16).astype(F32)
+        tail = jnp.concatenate(
+            [top, middle, b_up - top - middle, jnp.zeros((channels - 3, b_up.shape[1]), F32)], axis=0
+        )
+        up_ref[channels : 2 * channels, :] = tail.astype(BF16)
+        rows_ref[...] = jnp.zeros_like(rows_ref)
+
+    def fill():
+        lots = [(ref, n) for ref in maps_refs for n in range(ref.shape[0])]
+        for source, (ref, n) in enumerate(lots):
+            wide = ref[n].astype(F32)
+            for head in range(heads):
+                place = (source * heads + head) * block
+                rows_ref[place : place + block, 0:columns] = wide[
+                    :, head * columns : (head + 1) * columns
+                ]
+
+    gain, bias = gain_ref[...], bias_ref[...]
+
+    def normalise(g):
+        tall = jnp.concatenate(
+            [rows_ref[pl.ds(g * group + i, heads_all, stride=block), :] for i in range(group)], axis=0
+        )
+        flat = tall.T[0:columns].astype(BF16)
+        mixed = (
+            jnp.dot(
+                jnp.concatenate([flat, flat], axis=1), spread_ref[...], preferred_element_type=F32
+            )
+            + shift_ref[...]
+        )
+        pieces = []
+        for i in range(group):
+            centered = mixed[:, i * channels : (i + 1) * channels]
+            variance = jnp.sum(centered * centered, axis=1, keepdims=True) * (1.0 / channels)
+            pieces.append((centered * lax.rsqrt(variance + 1e-05) * gain + bias).astype(BF16))
+        return jnp.concatenate(pieces, axis=0)
+
+    lane = lax.broadcasted_iota(jnp.int32, (chunk, channels), 1)
+    unit = jnp.where(lane < 3, 1.0, 0.0).astype(BF16)
+
+    def transition(normed, at):
+        hidden = jnp.dot(
+            jnp.concatenate([normed, unit], axis=1), up_ref[...], preferred_element_type=F32
+        )
+        hidden = jnp.maximum(hidden, 0.0).astype(BF16)
+        result = jnp.dot(hidden, w_down_ref[...], preferred_element_type=F32) + b_down_ref[...]
+        result = result.astype(BF16)
+        for i in range(chunk // columns):
+            out_ref[at + i] = result[i * columns : (i + 1) * columns]
+
+    fill()
+    per = chunk // columns // group
+    waiting = None
+    for first in range(0, block // group, per):
+        normed = jnp.concatenate([normalise(g) for g in range(first, first + per)], axis=0)
+        if waiting is not None:
+            transition(*waiting)
+        waiting = (normed, first * group)
+    transition(*waiting)
+
+
+def pair_block_fast(
+    at,
+    maps,
+    w_maps,
+    b_maps,
+    pair_gain,
+    pair_bias,
+    w_up,
+    b_up,
+    w_down,
+    b_down,
+    factor,
+    columns,
+    block=64,
+    first=0,
+    blocks=None,
+    begun=None,
+):
+    count = sum(array.shape[0] for array in maps)
+    rows, wide = maps[0].shape[1:]
+    channels, hidden = w_up.shape
+    heads_all = w_maps.shape[0]
+    group = HD // heads_all
+    whole = lambda *shape: pl.BlockSpec(shape, lambda n: (0,) * len(shape))
+    blocks = rows // block if blocks is None else blocks
+    pairs = blocks * block * columns
+    chained = [] if begun is None else [begun]
+    return pl.pallas_call(
+        functools.partial(pair_kernel, factor, len(maps), count, len(chained)),
+        grid=(blocks,),
+        in_specs=[SMEM]
+        + [
+            pl.BlockSpec((array.shape[0], block, wide), lambda n: (0, first + n, 0))
+            for array in maps
+        ]
+        + [
+            whole(heads_all, channels),
+            whole(1, channels),
+            whole(1, channels),
+            whole(1, channels),
+            whole(channels, hidden),
+            whole(1, hidden),
+            whole(hidden, channels),
+            whole(1, channels),
+        ]
+        + [pl.BlockSpec(memory_space=pl.ANY)] * len(chained),
+        out_specs=pl.BlockSpec((block, columns, channels), lambda n: (first + n, 0, 0)),
+        out_shape=sds((rows, columns, channels), BF16),
+        scratch_shapes=[
+            pltpu.VMEM((2 * HD, group * channels), BF16),
+            pltpu.VMEM((2 * channels, hidden), BF16),
+            pltpu.VMEM((1, group * channels), F32),
+            pltpu.VMEM((heads_all * block, HD), F32),
+        ],
+        input_output_aliases={len(maps) + 9: 0} if chained else {},
+        compiler_params=params("arbitrary"),
+        cost_estimate=cost(4 * pairs * channels * hidden, 4 * pairs * channels, pairs * channels),
+        name="pair_block",
+    )(
+        at,
+        *maps,
+        w_maps,
+        b_maps.reshape(1, -1),
+        pair_gain.reshape(1, -1),
+        pair_bias.reshape(1, -1),
+        w_up,
+        b_up.reshape(1, -1),
+        w_down,
+        b_down.reshape(1, -1),
+        *chained,
+    )
+
+
+def per_device_fast(
+    layer_input,
+    norm_gain,
+    norm_bias,
+    w_query_key,
+    w_value,
+    w_out,
+    w_maps,
+    b_maps,
+    pair_gain,
+    pair_bias,
+    w_up,
+    b_up,
+    w_down,
+    b_down,
+):
+    rows = layer_input.shape[0]
+    parts = lax.axis_size("mp")
+    ring = parts // 2
+    tokens = rows * lax.axis_size("rows")
+    columns = tokens // parts
+    core = lax.axis_index("rows")
+    z, y = lax.axis_index("mp") // 2, lax.axis_index("mp") % 2
+
+    swap_core = [(0, 1), (1, 0)]
+    swap_y = [(m, m ^ 1) for m in range(parts)]
+
+    def rotate_z(by):
+        return [(2 * a + b, 2 * ((a + by) % ring) + b) for a in range(ring) for b in range(2)]
+
+    half = HD // 2
+    freqs = 10000.0 ** (-jnp.arange(half, dtype=F32) / half)
+    positions = core * rows + jnp.arange(rows, dtype=jnp.int32)
+    angles = positions.astype(F32)[:, None] * freqs[None, :]
+    at = jnp.stack([core, z, y]).astype(jnp.int32)
+
+    w_half = pack_columns(at, w_out, ring)
+    w_same = lax.ppermute(w_half, "mp", swap_y)
+    queries, own = project(
+        layer_input, norm_gain, norm_bias, w_query_key, w_value, jnp.cos(angles), jnp.sin(angles)
+    )
+    there = lax.ppermute(own, "rows", swap_core)
+    passed = [queries]
+    for _ in range(1, ring):
+        passed.append(lax.ppermute(passed[-1], "mp", rotate_z(1)))
+    near, local, *shares = attend(at, queries, own, there, ring, columns)
+    sources = [(queries, local)]
+    for d in range(1, ring):
+        mine = lax.ppermute(shares[d - 1], "mp", rotate_z(d))
+        theirs = lax.ppermute(mine, "rows", swap_core)
+        sources.append((passed[d], mine, theirs))
+    far = lax.ppermute(near, "mp", swap_y)
+    w_cross = lax.ppermute(w_same, "rows", swap_core)
+
+    own_maps, other_maps = [], []
+    for some in (sources[:-2], sources[-2:-1], sources[-1:]):
+        own_side, other_side = pair_maps(at, some, columns)
+        own_maps.append(own_side)
+        other_maps.append(lax.ppermute(other_side, "mp", swap_y))
+
+    total, *tails = project_out(at, near, far, w_out, w_same, w_cross, ring)
+    pair = functools.partial(
+        pair_block_fast,
+        at,
+        own_maps + other_maps,
+        w_maps,
+        b_maps,
+        pair_gain,
+        pair_bias,
+        w_up,
+        b_up,
+        w_down,
+        b_down,
+        float(tokens),
+        columns,
+    )
+    for tail in tails:
+        sent = total.astype(BF16)
+        total = tail + lax.ppermute(sent, "mp", rotate_z(1)).astype(F32)
+    attention = total
+    calls = 3
+    blocks = rows // 64
+    pair_features = None
+    for n in range(calls):
+        pair_features = pair(first=n * blocks // calls, blocks=blocks // calls, begun=pair_features)
+    return (attention, pair_features)
 
 
 def layer_norm(values, gain, bias):
@@ -120,6 +728,11 @@
         P(),
     )
     out_specs = (P(("groups", "rows"), "mp"), P(("groups", "rows"), "mp", None))
+    if mesh.shape["mp"] != 8 or mesh.shape["rows"] != 2:
+        return jax.shard_map(
+            per_device, mesh=mesh, in_specs=in_specs, out_specs=out_specs, check_vma=False
+        )
+
     return jax.shard_map(
-        per_device, mesh=mesh, in_specs=in_specs, out_specs=out_specs, check_vma=False
-    )
+        per_device_fast, mesh=mesh, in_specs=in_specs, out_specs=out_specs, check_vma=False
+    )

time: 283 us -> 172 us (0.61); the launches traced: 279 us -> 171 us
  blocking collectives: 123 us -> 0 us
  waiting for transfers between devices: 7.43 us -> 86.5 us
  matrix products: 62.7 us -> 0 us
  Pallas kernels: 0 us -> 59.5 us
  local copies, waits for them, and re-layouts: 49.7 us -> 4.66 us
  other arithmetic: 21.6 us -> 2.13 us
  starting transfers between devices: 0.04 us -> 17.6 us
  between operations: 14.6 us -> 0.92 us
    all_to_all x1 -> x0, blocking collectives: 117 us -> none  [per_device(): lax.all_to_all(maps, 'mp', split_axis=2, concat_axis=0, tiled=True)]
    ppermute x0 -> x19, waiting for transfers between devices: none -> 86.5 us  [the longest x1 28 us: per_device_fast(): w_same = lax.ppermute(w_half, 'mp', swap_y)]
    pallas_call x0 -> x10, Pallas kernels: none -> 59.5 us  [the longest x3 33.8 us: pair_block_fast(): pl.pallas_call(functools.partial(pair_kernel, factor, len(maps), count, l...]
    dot_general x7 -> x0, matrix products: 58.8 us -> none  [the longest x1 26.5 us: pair_block(): jnp.einsum('rct,tp->rcp', hidden, w_down, preferred_element_type=jnp.floa...]
    dot_general x3 -> x0, local copies, waits for them, and re-layouts: 24.7 us -> none  [project_rotated(): projected = jnp.dot(normed, weight, preferred_element_type=jnp.float32)]
    reduce_sum x3 -> x0, other arithmetic: 18 us -> none  [the longest x2 15.1 us: layer_norm(): variance = jnp.mean(centered * centered, axis=-1, keepdims=True)]
    ppermute x0 -> x19, starting transfers between devices: none -> 17.6 us  [the longest x3 4.32 us: per_device_fast(): mine = lax.ppermute(shares[d - 1], 'mp', rotate_z(d))]
    unnamed x27 -> x28, local copies, waits for them, and re-layouts: 13.9 us -> 4.66 us
  transfers between devices with their start and end apart: 1 -> 19, of which waited for: 1 -> 10; matrix products, arithmetic and copies ran while one was open for 24% -> 1% of each run, Pallas kernels for 0% -> 34%
where the time goes in v1:
time: 172 us; the launch traced here: 171 us
  waiting for transfers between devices  86.5 us (50%)
  Pallas kernels  59.5 us (35%)
  starting transfers between devices  17.6 us (10%)
  local copies, waits for them, and re-layouts  4.66 us (3%)
  other arithmetic  2.13 us (1%)
    pallas_call x3, Pallas kernels, pair_block_fast(): pl.pallas_call(functools.partial(pair_kernel, factor, len(maps), count, l...  33.8 us
    ppermute x1, waiting for transfers between devices, per_device_fast(): w_same = lax.ppermute(w_half, 'mp', swap_y)  28 us
    ppermute x3, waiting for transfers between devices, per_device_fast(): mine = lax.ppermute(shares[d - 1], 'mp', rotate_z(d))  25.3 us
    ppermute x3, waiting for transfers between devices, per_device_fast(): other_maps.append(lax.ppermute(other_side, 'mp', swap_y))  22 us
    pallas_call x1, Pallas kernels, project(): pl.pallas_call(project_kernel, in_specs=[HBM, VMEM, VMEM, HBM, HBM, VMEM,...  12.2 us
    ppermute x3, waiting for transfers between devices, per_device_fast(): passed.append(lax.ppermute(passed[-1], 'mp', rotate_z(1)))  7.12 us
    pallas_call x1, Pallas kernels, project_out(): pl.pallas_call(project_out_kernel, in_specs=[SMEM, VMEM, VMEM, ANYWHERE,...  4.78 us
    unnamed x28, local copies, waits for them, and re-layouts  4.66 us
  transfers between devices with their start and end apart: 19, of which 10 were waited for; matrix products, arithmetic and copies ran while one was open for 1% of the time, Pallas kernels for 34%

profile of v1, /device:TPU:0, one launch (start us, length us, event | category | flops | bytes accessed | tf_op | source)
XLA Modules:
  0.0 171.4 jit_solution(9364034472754460190)
XLA Ops:
  0.7 0.1 pad_add_fusion.at_ref
  0.7 2.5 %copy-done = bf16[512,5120]{1,0:T(8,128)(2,1)S(1)} copy-done((bf16[512,5120]{1,0:T(8,128)(2,1)S(1)}, bf16[512,5120]{1,0:T(8,128)(2,1)}, u32[]{:S(2)}) %copy-start) | copy-done | bytes 5242904
  3.2 0.7 pack_columns.1
  4.0 3.1 %collective-permute-start.2 = (bf16[256,2560]{1,0:T(8,128)(2,1)S(1)}, bf16[256,2560]{1,0:T(8,128)(2,1)S(1)}, u32[]{:S(2)}, u32[]{:S(2)}) collective-permute-start(bf16[256,2560]{1,0:T(8,128)(2,1)S(1)} %pack_columns.1), channel_id=1, source_target_pairs={{0,2},{2,0},{4,6},{6,4},{8,10},{10,8},{12,14},{14,12},{1,3},{3,1},... | collective-permute-start | bytes 3932168 | tf_op jit(solution)/shard_map/ppermute | solution.py:568
  7.1 0.8 multiply_sine_fusion
  7.8 28.0 %collective-permute-done.2.w_same_ref = bf16[256,2560]{1,0:T(8,128)(2,1)S(1)} collective-permute-done((bf16[256,2560]{1,0:T(8,128)(2,1)S(1)}, bf16[256,2560]{1,0:T(8,128)(2,1)S(1)}, u32[]{:S(2)}, u32[]{:S(2)}) %collective-permute-start.2) | collective-permute-done | bytes 1310752 | tf_op jit(solution)/shard_map/ppermute | solution.py:568
  35.8 0.0 copy-start.9
  35.8 2.1 %copy-done.9 = bf16[384,5120]{1,0:T(8,128)(2,1)S(1)} copy-done((bf16[384,5120]{1,0:T(8,128)(2,1)S(1)}, bf16[384,5120]{1,0:T(8,128)(2,1)}, u32[]{:S(2)}) %copy-start.9) | copy-done | bytes 3932184
  38.0 12.2 %project.1 = (bf16[384,512]{1,0:T(8,128)(2,1)S(1)}, bf16[384,1024]{1,0:T(8,128)(2,1)S(1)}) custom-call(bf16[384,5120]{1,0:T(8,128)(2,1)S(1)} %copy-done.9, f32[1,5120]{1,0:T(1,128)S(1)} %bitcast.27, f32[1,5120]{1,0:T(1,128)S(1)} %bitcast.28, bf16[2,5120,512]{2,1,0:T(8,128)(2,1)} %wqk_ref.1, bf16[5120,512]{1,0:T(8,128)(2,1)} %wv_ref.1, ...), custom_call_target="tpu_custom_call" | custom-call | flops 6039797760 | bytes 19660800 | tf_op jit(solution)/shard_map/project/pallas_call | solution.py:123
  50.2 0.6 collective-permute-start
  50.7 1.8 %collective-permute-start.7 = (bf16[384,512]{1,0:T(8,128)(2,1)S(1)}, bf16[384,512]{1,0:T(8,128)(2,1)S(1)}, u32[]{:S(2)}, u32[]{:S(2)}) collective-permute-start(bf16[384,512]{1,0:T(8,128)(2,1)S(1)} %get-tuple-element.19.q_ref.refs_0_), channel_id=1, source_target_pairs={{0,4},{2,6},{4,8},{6,10},{8,12},{10,14},{12,0},{14,2},{1,5},{3,7},... | collective-permute-start | bytes 1179656 | tf_op jit(solution)/shard_map/ppermute | solution.py:575
  52.5 0.1 collective-permute-done.there_ref
  52.6 3.8 %attend.1 = (bf16[384,512]{1,0:T(8,128)(2,1)S(1)}, bf16[208,512]{1,0:T(8,128)(2,1)S(1)}, bf16[112,512]{1,0:T(8,128)(2,1)S(1)}, bf16[112,512]{1,0:T(8,128)(2,1)S(1)}, bf16[112,512]{1,0:T(8,128)(2,1)S(1)}) custom-call(s32[3]{0:T(128)S(1)} %pad_add_fusion.at_ref, bf16[384,512]{1,0:T(8,128)(2,1)S(1)} %get-tuple-element.19.q_ref.refs_0_, ...), custom_call_target="tpu_custom_call" | custom-call | flops 603979776 | bytes 1572864 | tf_op jit(solution)/shard_map/attend/pallas_call | solution.py:199
  56.5 1.8 %collective-permute-start.1 = (bf16[384,512]{1,0:T(8,128)(2,1)S(1)}, bf16[384,512]{1,0:T(8,128)(2,1)S(1)}, u32[]{:S(2)}, u32[]{:S(2)}) collective-permute-start(bf16[384,512]{1,0:T(8,128)(2,1)S(1)} %get-tuple-element.21.near_ref), channel_id=1, source_target_pairs={{0,2},{2,0},{4,6},{6,4},{8,10},{10,8},{12,14},{14,12},{1,3},{3,1},... | collective-permute-start | bytes 1179656 | tf_op jit(solution)/shard_map/ppermute | solution.py:582
  58.3 5.6 %collective-permute-done.7.refs_2_ = bf16[384,512]{1,0:T(8,128)(2,1)S(1)} collective-permute-done((bf16[384,512]{1,0:T(8,128)(2,1)S(1)}, bf16[384,512]{1,0:T(8,128)(2,1)S(1)}, u32[]{:S(2)}, u32[]{:S(2)}) %collective-permute-start.7) | collective-permute-done | bytes 393248 | tf_op jit(solution)/shard_map/ppermute | solution.py:575
  63.9 4.0 %collective-permute-done.1.far_ref = bf16[384,512]{1,0:T(8,128)(2,1)S(1)} collective-permute-done((bf16[384,512]{1,0:T(8,128)(2,1)S(1)}, bf16[384,512]{1,0:T(8,128)(2,1)S(1)}, u32[]{:S(2)}, u32[]{:S(2)}) %collective-permute-start.1) | collective-permute-done | bytes 393248 | tf_op jit(solution)/shard_map/ppermute | solution.py:582
  68.0 4.8 %project_out.1 = (bf16[384,640]{1,0:T(8,128)(2,1)S(1)}, f32[384,640]{1,0:T(8,128)S(1)}, f32[384,640]{1,0:T(8,128)S(1)}, f32[384,640]{1,0:T(8,128)S(1)}) custom-call(s32[3]{0:T(128)S(1)} %pad_add_fusion.at_ref, bf16[384,512]{1,0:T(8,128)(2,1)S(1)} %get-tuple-element.21.near_ref, bf16[384,512]{1,0:T(8,128)(2,1)S(1)} %collective-permute-done.1.far_ref, ...), custom_call_target="tpu_custom_call" | custom-call | flops 2013265920 | bytes 9175040 | tf_op jit(solution)/shard_map/project_out/pallas_call | solution.py:281
  72.8 0.0 copy-start.3
  72.8 0.0 copy-start.4
  72.8 0.0 copy-start.6
  72.8 0.0 copy-start.7
  72.8 1.8 %collective-permute-start.4 = (bf16[384,640]{1,0:T(8,128)(2,1)S(1)}, bf16[384,640]{1,0:T(8,128)(2,1)S(1)}, u32[]{:S(2)}, u32[]{:S(2)}) collective-permute-start(bf16[384,640]{1,0:T(8,128)(2,1)S(1)} %get-tuple-element.25), channel_id=1, source_target_pairs={{0,4},{2,6},{4,8},{6,10},{8,12},{10,14},{12,0},{14,2},{1,5},{3,7},... | collective-permute-start | bytes 1474568 | tf_op jit(solution)/shard_map/ppermute | solution.py:609
  74.7 1.5 collective-permute-done.10.refs_0_
  76.2 0.1 collective-permute-start.13
  76.3 1.6 collective-permute-start.8
  77.9 2.2 %collective-permute-start.14 = (bf16[112,512]{1,0:T(8,128)(2,1)S(1)}, bf16[112,512]{1,0:T(8,128)(2,1)S(1)}, u32[]{:S(2)}, u32[]{:S(2)}) collective-permute-start(bf16[112,512]{1,0:T(8,128)(2,1)S(1)} %get-tuple-element.31), channel_id=1, source_target_pairs={{0,12},{2,14},{4,0},{6,2},{8,4},{10,6},{12,8},{14,10},{1,13},{3,15... | collective-permute-start | bytes 344072 | tf_op jit(solution)/shard_map/ppermute | solution.py:579
  80.1 0.5 collective-permute-start.11
  80.6 19.1 %collective-permute-done.8.refs_3_ = bf16[112,512]{1,0:T(8,128)(2,1)S(1)} collective-permute-done((bf16[112,512]{1,0:T(8,128)(2,1)S(1)}, bf16[112,512]{1,0:T(8,128)(2,1)S(1)}, u32[]{:S(2)}, u32[]{:S(2)}) %collective-permute-start.8) | collective-permute-done | bytes 114720 | tf_op jit(solution)/shard_map/ppermute | solution.py:579
  99.7 1.2 collective-permute-done.14.refs_1_
  101.0 0.0 collective-permute-start.15
  101.0 4.9 %collective-permute-done.11.refs_1_ = bf16[112,512]{1,0:T(8,128)(2,1)S(1)} collective-permute-done((bf16[112,512]{1,0:T(8,128)(2,1)S(1)}, bf16[112,512]{1,0:T(8,128)(2,1)S(1)}, u32[]{:S(2)}, u32[]{:S(2)}) %collective-permute-start.11) | collective-permute-done | bytes 114720 | tf_op jit(solution)/shard_map/ppermute | solution.py:579
  105.9 0.0 collective-permute-start.12
  105.9 1.7 %pair_maps.3 = (bf16[2,384,384]{2,1,0:T(8,128)(2,1)S(1)}, bf16[2,384,384]{2,1,0:T(8,128)(2,1)S(1)}) custom-call(s32[3]{0:T(128)S(1)} %pad_add_fusion.at_ref, bf16[384,512]{1,0:T(8,128)(2,1)S(1)} %get-tuple-element.19.q_ref.refs_0_, bf16[208,512]{1,0:T(8,128)(2,1)S(1)} %get-tuple-element.26.refs_1_, bf16[384,512]{1,0:T(8,128)(2,1)S(1)} %collective-permute-done.7.refs_2_, ...), custom_call_target="tpu_custom_call" | custom-call | flops 603979776 | bytes 2359296 | tf_op jit(solution)/shard_map/pair_maps/pallas_call | solution.py:345
  107.7 1.6 collective-permute-start.16
  109.2 1.2 pair_maps.4
  110.5 0.6 collective-permute-start.17
  111.1 1.2 pair_maps.5
  112.3 1.6 collective-permute-start.18
  113.9 0.1 add_convert_fusion.1
  114.0 0.1 collective-permute-start.5
  114.1 16.1 %collective-permute-done.17.refs_4_ = bf16[1,384,384]{2,1,0:T(8,128)(2,1)S(1)} collective-permute-done((bf16[1,384,384]{2,1,0:T(8,128)(2,1)S(1)}, bf16[1,384,384]{2,1,0:T(8,128)(2,1)S(1)}, u32[]{:S(2)}, u32[]{:S(2)}) %collective-permute-start.17) | collective-permute-done | bytes 294944 | tf_op jit(solution)/shard_map/ppermute | solution.py:589
  130.2 5.8 %collective-permute-done.18.refs_5_ = bf16[1,384,384]{2,1,0:T(8,128)(2,1)S(1)} collective-permute-done((bf16[1,384,384]{2,1,0:T(8,128)(2,1)S(1)}, bf16[1,384,384]{2,1,0:T(8,128)(2,1)S(1)}, u32[]{:S(2)}, u32[]{:S(2)}) %collective-permute-start.18) | collective-permute-done | bytes 294944 | tf_op jit(solution)/shard_map/ppermute | solution.py:589
  136.2 11.3 %pair_block.3.refs_14_ = bf16[384,96,128]{2,1,0:T(8,128)(2,1)} custom-call(s32[3]{0:T(128)S(1)} %pad_add_fusion.at_ref, bf16[2,384,384]{2,1,0:T(8,128)(2,1)S(1)} %get-tuple-element.28.refs_0_, bf16[1,384,384]{2,1,0:T(8,128)(2,1)S(1)} %get-tuple-element.30.refs_1_, bf16[1,384,384]{2,1,0:T(8,128)(2,1)S(1)} %get-tuple-element.32.refs_2_, ...), custom_call_target="tpu_custom_call" | custom-call | flops 3221225472 | bytes 6291456 | tf_op jit(solution)/shard_map/pair_block/pallas_call | solution.py:485
  147.4 0.1 add_convert_fusion
  147.5 0.3 collective-permute-start.6
  147.8 11.3 %pair_block.4.refs_14_ = bf16[384,96,128]{2,1,0:T(8,128)(2,1)} custom-call(s32[3]{0:T(128)S(1)} %pad_add_fusion.at_ref, bf16[2,384,384]{2,1,0:T(8,128)(2,1)S(1)} %get-tuple-element.28.refs_0_, bf16[1,384,384]{2,1,0:T(8,128)(2,1)S(1)} %get-tuple-element.30.refs_1_, ...), custom_call_target="tpu_custom_call", output_to_operand_aliasing={{}: (15, {})} | custom-call | flops 3221225472 | bytes 6291456 | tf_op jit(solution)/shard_map/pair_block/pallas_call | solution.py:485
  159.1 11.2 %pair_block.5 = bf16[384,96,128]{2,1,0:T(8,128)(2,1)} custom-call(s32[3]{0:T(128)S(1)} %pad_add_fusion.at_ref, bf16[2,384,384]{2,1,0:T(8,128)(2,1)S(1)} %get-tuple-element.28.refs_0_, bf16[1,384,384]{2,1,0:T(8,128)(2,1)S(1)} %get-tuple-element.30.refs_1_, bf16[1,384,384]{2,1,0:T(8,128)(2,1)S(1)} %get-tuple-element.32.refs_2_, ...), custom_call_target="tpu_custom_call", output_to_operand_aliasing={{}: (15, {})} | custom-call | flops 3221225472 | bytes 6291456 | tf_op jit(solution)/shard_map/pair_block/pallas_call | solution.py:485
  170.3 1.1 convert_add_fusion
  (36 shorter events, 0.1 us)
Async XLA Ops:
  0.6 35.2 %copy-start.10 = (f32[5120]{0:T(1024)S(1)}, f32[5120]{0:T(1024)}, u32[]{:S(2)}) copy-start(f32[5120]{0:T(1024)} %param.15) | copy-start | bytes 61444
  0.6 35.2 %copy-start.11 = (f32[5120]{0:T(1024)S(1)}, f32[5120]{0:T(1024)}, u32[]{:S(2)}) copy-start(f32[5120]{0:T(1024)} %param.16) | copy-start | bytes 61444
  0.7 2.5 %copy-start = (bf16[512,5120]{1,0:T(8,128)(2,1)S(1)}, bf16[512,5120]{1,0:T(8,128)(2,1)}, u32[]{:S(2)}) copy-start(bf16[512,5120]{1,0:T(8,128)(2,1)} %w_ref.3) | copy-start | bytes 15728644
  4.0 31.8 %collective-permute-start.2 = (bf16[256,2560]{1,0:T(8,128)(2,1)S(1)}, bf16[256,2560]{1,0:T(8,128)(2,1)S(1)}, u32[]{:S(2)}, u32[]{:S(2)}) collective-permute-start(bf16[256,2560]{1,0:T(8,128)(2,1)S(1)} %pack_columns.1), channel_id=1, source_target_pairs={{0,2},{2,0},{4,6},{6,4},{8,10},{10,8},{12,14},{14,12},{1,3},{3,1},... | collective-permute-start | bytes 3932168 | tf_op jit(solution)/shard_map/ppermute | solution.py:568
  7.1 60.9 %slice-start = ((s8[5242880]{0:T(1024)(128)(4,1)}), s8[4194304]{0:T(1024)(128)(4,1)S(1)}, s32[]{:S(2)}) async-start(s8[5242880]{0:T(1024)(128)(4,1)} %bitcast.10), calls=%async_computation | async-start | bytes 8388608
  35.8 32.1 %collective-permute-start.3 = (bf16[256,2560]{1,0:T(8,128)(2,1)S(1)}, bf16[256,2560]{1,0:T(8,128)(2,1)S(1)}, u32[]{:S(2)}, u32[]{:S(2)}) collective-permute-start(bf16[256,2560]{1,0:T(8,128)(2,1)S(1)} %collective-permute-done.2.w_same_ref), channel_id=1, source_target_pairs={{0,1},{1,0},{2,3},{3,2},{4,5},{5,4},{6,7},{7,6},{8,9},{9,8},{10,11... | collective-permute-start | bytes 3932168 | tf_op jit(solution)/shard_map/ppermute | solution.py:583
  35.8 2.1 %copy-start.9 = (bf16[384,5120]{1,0:T(8,128)(2,1)S(1)}, bf16[384,5120]{1,0:T(8,128)(2,1)}, u32[]{:S(2)}) copy-start(bf16[384,5120]{1,0:T(8,128)(2,1)} %x_ref.1) | copy-start | bytes 11796484
  38.0 30.0 %slice-start.1 = ((s8[5242880]{0:T(1024)(128)(4,1)}), s8[1048576]{0:T(1024)(128)(4,1)S(1)}, s32[]{:S(2)}) async-start(s8[5242880]{0:T(1024)(128)(4,1)} %bitcast.10), calls=%async_computation.1 | async-start | bytes 2097152
  50.2 2.5 %collective-permute-start = (bf16[384,1024]{1,0:T(8,128)(2,1)S(1)}, bf16[384,1024]{1,0:T(8,128)(2,1)S(1)}, u32[]{:S(2)}, u32[]{:S(2)}) collective-permute-start(bf16[384,1024]{1,0:T(8,128)(2,1)S(1)} %get-tuple-element.20.own_ref), channel_id=1, source_target_pairs={{0,1},{1,0},{2,3},{3,2},{4,5},{5,4},{6,7},{7,6},{8,9},{9,8},{10,11... | collective-permute-start | bytes 2359304 | tf_op jit(solution)/shard_map/ppermute | solution.py:572
  50.7 13.2 %collective-permute-start.7 = (bf16[384,512]{1,0:T(8,128)(2,1)S(1)}, bf16[384,512]{1,0:T(8,128)(2,1)S(1)}, u32[]{:S(2)}, u32[]{:S(2)}) collective-permute-start(bf16[384,512]{1,0:T(8,128)(2,1)S(1)} %get-tuple-element.19.q_ref.refs_0_), channel_id=1, source_target_pairs={{0,4},{2,6},{4,8},{6,10},{8,12},{10,14},{12,0},{14,2},{1,5},{3,7},... | collective-permute-start | bytes 1179656 | tf_op jit(solution)/shard_map/ppermute | solution.py:575
  56.5 11.5 %collective-permute-start.1 = (bf16[384,512]{1,0:T(8,128)(2,1)S(1)}, bf16[384,512]{1,0:T(8,128)(2,1)S(1)}, u32[]{:S(2)}, u32[]{:S(2)}) collective-permute-start(bf16[384,512]{1,0:T(8,128)(2,1)S(1)} %get-tuple-element.21.near_ref), channel_id=1, source_target_pairs={{0,2},{2,0},{4,6},{6,4},{8,10},{10,8},{12,14},{14,12},{1,3},{3,1},... | collective-permute-start | bytes 1179656 | tf_op jit(solution)/shard_map/ppermute | solution.py:582
  63.9 12.3 %collective-permute-start.10 = (bf16[384,512]{1,0:T(8,128)(2,1)S(1)}, bf16[384,512]{1,0:T(8,128)(2,1)S(1)}, u32[]{:S(2)}, u32[]{:S(2)}) collective-permute-start(bf16[384,512]{1,0:T(8,128)(2,1)S(1)} %collective-permute-done.7.refs_2_), channel_id=1, source_target_pairs={{0,4},{2,6},{4,8},{6,10},{8,12},{10,14},{12,0},{14,2},{1,5},{3,7},... | collective-permute-start | bytes 1179656 | tf_op jit(solution)/shard_map/ppermute | solution.py:575
  72.8 63.3 %copy-start.1 = (bf16[128,512]{1,0:T(8,128)(2,1)S(1)}, bf16[128,512]{1,0:T(8,128)(2,1)}, u32[]{:S(2)}) copy-start(bf16[128,512]{1,0:T(8,128)(2,1)} %refs_10_.5) | copy-start | bytes 393220
  72.8 63.3 %copy-start.2 = (bf16[512,128]{1,0:T(8,128)(2,1)S(1)}, bf16[512,128]{1,0:T(8,128)(2,1)}, u32[]{:S(2)}) copy-start(bf16[512,128]{1,0:T(8,128)(2,1)} %refs_12_.5) | copy-start | bytes 393220
  72.8 63.3 %copy-start.3 = (bf16[32,128]{1,0:T(8,128)(2,1)S(1)}, bf16[32,128]{1,0:T(8,128)(2,1)}, u32[]{:S(2)}) copy-start(bf16[32,128]{1,0:T(8,128)(2,1)} %refs_6_.5) | copy-start | bytes 24580
  72.8 63.3 %copy-start.4 = (f32[512]{0:T(512)S(1)}, f32[512]{0:T(512)}, u32[]{:S(2)}) copy-start(f32[512]{0:T(512)} %param.25) | copy-start | bytes 6148
  72.8 63.3 %copy-start.5 = (f32[128]{0:T(128)S(1)}, f32[128]{0:T(128)}, u32[]{:S(2)}) copy-start(f32[128]{0:T(128)} %param.21) | copy-start | bytes 1540
  72.8 63.3 %copy-start.6 = (f32[128]{0:T(128)S(1)}, f32[128]{0:T(128)}, u32[]{:S(2)}) copy-start(f32[128]{0:T(128)} %param.22) | copy-start | bytes 1540
  72.8 63.3 %copy-start.7 = (f32[128]{0:T(128)S(1)}, f32[128]{0:T(128)}, u32[]{:S(2)}) copy-start(f32[128]{0:T(128)} %param.23) | copy-start | bytes 1540
  72.8 63.3 %copy-start.8 = (f32[128]{0:T(128)S(1)}, f32[128]{0:T(128)}, u32[]{:S(2)}) copy-start(f32[128]{0:T(128)} %param.27) | copy-start | bytes 1540
  72.8 41.1 %collective-permute-start.4 = (bf16[384,640]{1,0:T(8,128)(2,1)S(1)}, bf16[384,640]{1,0:T(8,128)(2,1)S(1)}, u32[]{:S(2)}, u32[]{:S(2)}) collective-permute-start(bf16[384,640]{1,0:T(8,128)(2,1)S(1)} %get-tuple-element.25), channel_id=1, source_target_pairs={{0,4},{2,6},{4,8},{6,10},{8,12},{10,14},{12,0},{14,2},{1,5},{3,7},... | collective-permute-start | bytes 1474568 | tf_op jit(solution)/shard_map/ppermute | solution.py:609
  76.2 34.9 %collective-permute-start.13 = (bf16[384,512]{1,0:T(8,128)(2,1)S(1)}, bf16[384,512]{1,0:T(8,128)(2,1)S(1)}, u32[]{:S(2)}, u32[]{:S(2)}) collective-permute-start(bf16[384,512]{1,0:T(8,128)(2,1)S(1)} %collective-permute-done.10.refs_0_), channel_id=1, source_target_pairs={{0,4},{2,6},{4,8},{6,10},{8,12},{10,14},{12,0},{14,2},{1,5},{3,7},... | collective-permute-start | bytes 1179656 | tf_op jit(solution)/shard_map/ppermute | solution.py:575
  76.3 23.5 %collective-permute-start.8 = (bf16[112,512]{1,0:T(8,128)(2,1)S(1)}, bf16[112,512]{1,0:T(8,128)(2,1)S(1)}, u32[]{:S(2)}, u32[]{:S(2)}) collective-permute-start(bf16[112,512]{1,0:T(8,128)(2,1)S(1)} %get-tuple-element.27), channel_id=1, source_target_pairs={{0,4},{2,6},{4,8},{6,10},{8,12},{10,14},{12,0},{14,2},{1,5},{3,7},... | collective-permute-start | bytes 344072 | tf_op jit(solution)/shard_map/ppermute | solution.py:579
  77.9 23.1 %collective-permute-start.14 = (bf16[112,512]{1,0:T(8,128)(2,1)S(1)}, bf16[112,512]{1,0:T(8,128)(2,1)S(1)}, u32[]{:S(2)}, u32[]{:S(2)}) collective-permute-start(bf16[112,512]{1,0:T(8,128)(2,1)S(1)} %get-tuple-element.31), channel_id=1, source_target_pairs={{0,12},{2,14},{4,0},{6,2},{8,4},{10,6},{12,8},{14,10},{1,13},{3,15... | collective-permute-start | bytes 344072 | tf_op jit(solution)/shard_map/ppermute | solution.py:579
  80.1 25.8 %collective-permute-start.11 = (bf16[112,512]{1,0:T(8,128)(2,1)S(1)}, bf16[112,512]{1,0:T(8,128)(2,1)S(1)}, u32[]{:S(2)}, u32[]{:S(2)}) collective-permute-start(bf16[112,512]{1,0:T(8,128)(2,1)S(1)} %get-tuple-element.29), channel_id=1, source_target_pairs={{0,8},{2,10},{4,12},{6,14},{8,0},{10,2},{12,4},{14,6},{1,9},{3,11}... | collective-permute-start | bytes 344072 | tf_op jit(solution)/shard_map/ppermute | solution.py:579
  99.7 6.2 %collective-permute-start.9 = (bf16[112,512]{1,0:T(8,128)(2,1)S(1)}, bf16[112,512]{1,0:T(8,128)(2,1)S(1)}, u32[]{:S(2)}, u32[]{:S(2)}) collective-permute-start(bf16[112,512]{1,0:T(8,128)(2,1)S(1)} %collective-permute-done.8.refs_3_), channel_id=1, source_target_pairs={{0,1},{1,0},{2,3},{3,2},{4,5},{5,4},{6,7},{7,6},{8,9},{9,8},{10,11... | collective-permute-start | bytes 344072 | tf_op jit(solution)/shard_map/ppermute | solution.py:580
  101.0 10.1 %collective-permute-start.15 = (bf16[112,512]{1,0:T(8,128)(2,1)S(1)}, bf16[112,512]{1,0:T(8,128)(2,1)S(1)}, u32[]{:S(2)}, u32[]{:S(2)}) collective-permute-start(bf16[112,512]{1,0:T(8,128)(2,1)S(1)} %collective-permute-done.14.refs_1_), channel_id=1, source_target_pairs={{0,1},{1,0},{2,3},{3,2},{4,5},{5,4},{6,7},{7,6},{8,9},{9,8},{10,11... | collective-permute-start | bytes 344072 | tf_op jit(solution)/shard_map/ppermute | solution.py:580
  105.9 3.3 %collective-permute-start.12 = (bf16[112,512]{1,0:T(8,128)(2,1)S(1)}, bf16[112,512]{1,0:T(8,128)(2,1)S(1)}, u32[]{:S(2)}, u32[]{:S(2)}) collective-permute-start(bf16[112,512]{1,0:T(8,128)(2,1)S(1)} %collective-permute-done.11.refs_1_), channel_id=1, source_target_pairs={{0,1},{1,0},{2,3},{3,2},{4,5},{5,4},{6,7},{7,6},{8,9},{9,8},{10,11... | collective-permute-start | bytes 344072 | tf_op jit(solution)/shard_map/ppermute | solution.py:580
  107.7 28.4 %collective-permute-start.16 = (bf16[2,384,384]{2,1,0:T(8,128)(2,1)S(1)}, bf16[2,384,384]{2,1,0:T(8,128)(2,1)S(1)}, u32[]{:S(2)}, u32[]{:S(2)}) collective-permute-start(bf16[2,384,384]{2,1,0:T(8,128)(2,1)S(1)} %get-tuple-element.33), channel_id=1, source_target_pairs={{0,2},{2,0},{4,6},{6,4},{8,10},{10,8},{12,14},{14,12},{1,3},{3,1},... | collective-permute-start | bytes 1769480 | tf_op jit(solution)/shard_map/ppermute | solution.py:589
  110.5 19.8 %collective-permute-start.17 = (bf16[1,384,384]{2,1,0:T(8,128)(2,1)S(1)}, bf16[1,384,384]{2,1,0:T(8,128)(2,1)S(1)}, u32[]{:S(2)}, u32[]{:S(2)}) collective-permute-start(bf16[1,384,384]{2,1,0:T(8,128)(2,1)S(1)} %get-tuple-element.34), channel_id=1, source_target_pairs={{0,2},{2,0},{4,6},{6,4},{8,10},{10,8},{12,14},{14,12},{1,3},{3,1},... | collective-permute-start | bytes 884744 | tf_op jit(solution)/shard_map/ppermute | solution.py:589
  112.3 23.8 %collective-permute-start.18 = (bf16[1,384,384]{2,1,0:T(8,128)(2,1)S(1)}, bf16[1,384,384]{2,1,0:T(8,128)(2,1)S(1)}, u32[]{:S(2)}, u32[]{:S(2)}) collective-permute-start(bf16[1,384,384]{2,1,0:T(8,128)(2,1)S(1)} %get-tuple-element.35), channel_id=1, source_target_pairs={{0,2},{2,0},{4,6},{6,4},{8,10},{10,8},{12,14},{14,12},{1,3},{3,1},... | collective-permute-start | bytes 884744 | tf_op jit(solution)/shard_map/ppermute | solution.py:589
  114.0 33.4 %collective-permute-start.5 = (bf16[384,640]{1,0:T(8,128)(2,1)S(1)}, bf16[384,640]{1,0:T(8,128)(2,1)S(1)}, u32[]{:S(2)}, u32[]{:S(2)}) collective-permute-start(bf16[384,640]{1,0:T(8,128)(2,1)S(1)} %add_convert_fusion.1), channel_id=1, source_target_pairs={{0,4},{2,6},{4,8},{6,10},{8,12},{10,14},{12,0},{14,2},{1,5},{3,7},... | collective-permute-start | bytes 1474568 | tf_op jit(solution)/shard_map/ppermute | solution.py:609
  147.5 22.8 %collective-permute-start.6 = (bf16[384,640]{1,0:T(8,128)(2,1)S(1)}, bf16[384,640]{1,0:T(8,128)(2,1)S(1)}, u32[]{:S(2)}, u32[]{:S(2)}) collective-permute-start(bf16[384,640]{1,0:T(8,128)(2,1)S(1)} %add_convert_fusion), channel_id=1, source_target_pairs={{0,4},{2,6},{4,8},{6,10},{8,12},{10,14},{12,0},{14,2},{1,5},{3,7},... | collective-permute-start | bytes 1474568 | tf_op jit(solution)/shard_map/ppermute | solution.py:609

commit v2 on v1

--- a/solution.py
+++ b/solution.py
@@ -214,18 +214,20 @@
     tile = wide // count
     core, z, y = at_ref[0], at_ref[1], at_ref[2]
     copies = []
+    piece = depth // sems.shape[1]
     for n in range(count):
         block = 2 * lax.rem(z + (2 * count - 1 - n), count) + 1 - y
-        copies.append(
-            pltpu.make_async_copy(
-                w_ref.at[
-                    pl.ds(pl.multiple_of(core * depth, depth), depth),
-                    pl.ds(pl.multiple_of(block * tile, tile), tile),
-                ],
-                out_ref.at[:, n * tile : (n + 1) * tile],
-                sems.at[n],
+        for part in range(sems.shape[1]):
+            copies.append(
+                pltpu.make_async_copy(
+                    w_ref.at[
+                        pl.ds(pl.multiple_of(core * depth + part * piece, piece), piece),
+                        pl.ds(pl.multiple_of(block * tile, tile), tile),
+                    ],
+                    out_ref.at[part * piece : (part + 1) * piece, n * tile : (n + 1) * tile],
+                    sems.at[n, part],
+                )
             )
-        )
     for copy in copies:
         copy.start()
     for copy in copies:
@@ -239,7 +241,7 @@
         in_specs=[SMEM, HBM],
         out_specs=VMEM,
         out_shape=sds((depth, wide), BF16),
-        scratch_shapes=[pltpu.SemaphoreType.DMA((count,))],
+        scratch_shapes=[pltpu.SemaphoreType.DMA((count, 4))],
         compiler_params=params(),
         cost_estimate=cost(0, 4 * depth * wide),
         name="pack_columns",
@@ -293,7 +295,7 @@
     )(at, near, far, w, w_same, w_cross)
 
 
-def pair_maps_kernel(sources, at_ref, *refs):
+def pair_maps_kernel(sources, first, at_ref, *refs):
     own_ref, other_ref = refs[-2:]
     rows = own_ref.shape[1]
     width = refs[0].shape[1]
@@ -315,7 +317,7 @@
         taken += count
         if count == 2:
             pieces = [keys[0][n * columns : (n + 1) * columns, :].astype(F32) for n in range(2)]
-            levels = keys[0][2 * columns : 2 * columns + 16, 0:rows]
+            levels = keys[0][2 * columns : 2 * columns + 16, first : first + rows]
         else:
             mine = keys[0][0:columns, :].astype(F32)
             theirs = keys[1][0:columns, :].astype(F32)
@@ -323,7 +325,7 @@
                 mine * straight + theirs * (1.0 - straight),
                 theirs * straight + mine * (1.0 - straight),
             ]
-            levels = keys[0][columns : columns + 16, 0:rows]
+            levels = keys[0][columns : columns + 16, first : first + rows]
         level = lax.dot_general(
             levels, pick, (((0,), (0,)), ((), ())), preferred_element_type=F32
         )
@@ -337,13 +339,13 @@
             out_ref[place] = jnp.exp((scores + level) * (1.0 / ROOT)).astype(BF16)
 
 
-def pair_maps(at, sources, columns):
+def pair_maps(at, sources, columns, first=0):
     rows, width = sources[0][0].shape
     wide = (width // HD) * columns
     count = len(sources)
     flat = [array for source in sources for array in source]
     return pl.pallas_call(
-        functools.partial(pair_maps_kernel, [len(source) for source in sources]),
+        functools.partial(pair_maps_kernel, [len(source) for source in sources], first),
         in_specs=[SMEM] + [VMEM] * len(flat),
         out_specs=[VMEM] * 2,
         out_shape=[sds((count, rows, wide), BF16)] * 2,
@@ -473,8 +475,8 @@
     blocks=None,
     begun=None,
 ):
-    count = sum(array.shape[0] for array in maps)
-    rows, wide = maps[0].shape[1:]
+    count = sum(array.shape[0] for array, _ in maps)
+    rows, wide = maps[0][0].shape[1:]
     channels, hidden = w_up.shape
     heads_all = w_maps.shape[0]
     group = HD // heads_all
@@ -487,8 +489,11 @@
         grid=(blocks,),
         in_specs=[SMEM]
         + [
-            pl.BlockSpec((array.shape[0], block, wide), lambda n: (0, first + n, 0))
-            for array in maps
+            pl.BlockSpec(
+                (array.shape[0], block, wide),
+                lambda n, skipped=skipped: (0, first + n - skipped // block, 0),
+            )
+            for array, skipped in maps
         ]
         + [
             whole(heads_all, channels),
@@ -515,7 +520,7 @@
         name="pair_block",
     )(
         at,
-        *maps,
+        *[array for array, _ in maps],
         w_maps,
         b_maps.reshape(1, -1),
         pair_gain.reshape(1, -1),
@@ -571,48 +576,60 @@
     )
     there = lax.ppermute(own, "rows", swap_core)
     passed = [queries]
-    for _ in range(1, ring):
+    for _ in range(1, ring - 1):
         passed.append(lax.ppermute(passed[-1], "mp", rotate_z(1)))
+    calls = 3
+    cut = rows // calls
+    last = [lax.ppermute(part, "mp", rotate_z(1)) for part in (passed[-1][:cut], passed[-1][cut:])]
     near, local, *shares = attend(at, queries, own, there, ring, columns)
     sources = [(queries, local)]
     for d in range(1, ring):
         mine = lax.ppermute(shares[d - 1], "mp", rotate_z(d))
         theirs = lax.ppermute(mine, "rows", swap_core)
-        sources.append((passed[d], mine, theirs))
+        if d < ring - 1:
+            sources.append((passed[d], mine, theirs))
     far = lax.ppermute(near, "mp", swap_y)
     w_cross = lax.ppermute(w_same, "rows", swap_core)
 
     own_maps, other_maps = [], []
-    for some in (sources[:-2], sources[-2:-1], sources[-1:]):
-        own_side, other_side = pair_maps(at, some, columns)
-        own_maps.append(own_side)
-        other_maps.append(lax.ppermute(other_side, "mp", swap_y))
+    for some, start in (
+        (sources[:-1], 0),
+        (sources[-1:], 0),
+        ([(last[0], mine, theirs)], 0),
+        ([(last[1], mine, theirs)], cut),
+    ):
+        own_side, other_side = pair_maps(at, some, columns, start)
+        own_maps.append((own_side, start))
+        other_maps.append((lax.ppermute(other_side, "mp", swap_y), start))
 
     total, *tails = project_out(at, near, far, w_out, w_same, w_cross, ring)
     pair = functools.partial(
         pair_block_fast,
         at,
-        own_maps + other_maps,
-        w_maps,
-        b_maps,
-        pair_gain,
-        pair_bias,
-        w_up,
-        b_up,
-        w_down,
-        b_down,
-        float(tokens),
-        columns,
+        w_maps=w_maps,
+        b_maps=b_maps,
+        pair_gain=pair_gain,
+        pair_bias=pair_bias,
+        w_up=w_up,
+        b_up=b_up,
+        w_down=w_down,
+        b_down=b_down,
+        factor=float(tokens),
+        columns=columns,
     )
     for tail in tails:
         sent = total.astype(BF16)
         total = tail + lax.ppermute(sent, "mp", rotate_z(1)).astype(F32)
     attention = total
-    calls = 3
     blocks = rows // 64
     pair_features = None
     for n in range(calls):
-        pair_features = pair(first=n * blocks // calls, blocks=blocks // calls, begun=pair_features)
+        pair_features = pair(
+            [side[k] for side in (own_maps, other_maps) for k in (0, 1, 2 if n == 0 else 3)],
+            first=n * blocks // calls,
+            blocks=blocks // calls,
+            begun=pair_features,
+        )
     return (attention, pair_features)
 
 

time: 172 us -> 166 us (0.965)
  waiting for transfers between devices: 86.5 us -> 77.8 us
    ppermute x3 -> x2, waiting for transfers between devices: 7.12 us -> 0.01 us  [per_device_fast(): passed.append(lax.ppermute(passed[-1], 'mp', rotate_z(1)))]
    ppermute x3 -> x6, waiting for transfers between devices: 22 us -> 16.4 us  [the longest x2 8.8 us: per_device_fast(): lax.ppermute(part, 'mp', rotate_z(1))]
    ppermute x1, waiting for transfers between devices: 4.04 us -> 8.07 us  [per_device_fast(): far = lax.ppermute(near, 'mp', swap_y)]
    ppermute x3, waiting for transfers between devices: 25.3 us -> 23.4 us  [per_device_fast(): mine = lax.ppermute(shares[d - 1], 'mp', rotate_z(d))]
    ppermute x1, waiting for transfers between devices: 0.11 us -> 1.91 us  [per_device_fast(): there = lax.ppermute(own, 'rows', swap_core)]
    ppermute x3 -> x6, starting transfers between devices: 3.73 us -> 4.74 us  [the longest x4 3.32 us: per_device_fast(): other_maps.append((lax.ppermute(other_side, 'mp', swap_y), start))]
    pallas_call x3 -> x4, Pallas kernels: 4.23 us -> 5.05 us  [pair_maps(): pl.pallas_call(functools.partial(pair_maps_kernel, [len(source) for sourc...]
  transfers between devices with their start and end apart: 19 -> 21, of which waited for: 10 -> 8; matrix products, arithmetic and copies ran while one was open for 1% -> 1% of each run, Pallas kernels for 34% -> 36%
where the time goes in v2:
time: 166 us
  waiting for transfers between devices  77.8 us (47%)
  Pallas kernels  60.7 us (37%)
  starting transfers between devices  19.2 us (12%)
  local copies, waits for them, and re-layouts  4.69 us (3%)
  other arithmetic  2.13 us (1%)
    pallas_call x3, Pallas kernels, pair_block_fast(): pl.pallas_call(functools.partial(pair_kernel, factor, len(maps), count, l...  33.9 us
    ppermute x1, waiting for transfers between devices, per_device_fast(): w_same = lax.ppermute(w_half, 'mp', swap_y)  28 us
    ppermute x3, waiting for transfers between devices, per_device_fast(): mine = lax.ppermute(shares[d - 1], 'mp', rotate_z(d))  23.4 us
    pallas_call x1, Pallas kernels, project(): pl.pallas_call(project_kernel, in_specs=[HBM, VMEM, VMEM, HBM, HBM, VMEM,...  12.2 us
    ppermute x2, waiting for transfers between devices, per_device_fast(): lax.ppermute(part, 'mp', rotate_z(1))  8.8 us
    ppermute x1, waiting for transfers between devices, per_device_fast(): far = lax.ppermute(near, 'mp', swap_y)  8.07 us
    ppermute x4, waiting for transfers between devices, per_device_fast(): other_maps.append((lax.ppermute(other_side, 'mp', swap_y), start))  7.62 us
    pallas_call x4, Pallas kernels, pair_maps(): pl.pallas_call(functools.partial(pair_maps_kernel, [len(source) for sourc...  5.05 us
  transfers between devices with their start and end apart: 21, of which 8 were waited for; matrix products, arithmetic and copies ran while one was open for 1% of the time, Pallas kernels for 36%

profile of v2, /device:TPU:0, one launch (start us, length us, event | category | flops | bytes accessed | tf_op | source)
XLA Modules:
  0.0 165.6 jit_solution(9309870579793394559)
XLA Ops:
  0.7 0.1 pad_add_fusion.at_ref
  0.7 2.5 %copy-done = bf16[512,5120]{1,0:T(8,128)(2,1)S(1)} copy-done((bf16[512,5120]{1,0:T(8,128)(2,1)S(1)}, bf16[512,5120]{1,0:T(8,128)(2,1)}, u32[]{:S(2)}) %copy-start) | copy-done | bytes 5242904
  3.2 1.0 pack_columns.1
  4.2 3.1 %collective-permute-start.2 = (bf16[256,2560]{1,0:T(8,128)(2,1)S(1)}, bf16[256,2560]{1,0:T(8,128)(2,1)S(1)}, u32[]{:S(2)}, u32[]{:S(2)}) collective-permute-start(bf16[256,2560]{1,0:T(8,128)(2,1)S(1)} %pack_columns.1), channel_id=1, source_target_pairs={{0,2},{2,0},{4,6},{6,4},{8,10},{10,8},{12,14},{14,12},{1,3},{3,1},... | collective-permute-start | bytes 3932168 | tf_op jit(solution)/shard_map/ppermute | solution.py:573
  7.3 0.8 multiply_sine_fusion
  8.1 28.0 %collective-permute-done.2.w_same_ref = bf16[256,2560]{1,0:T(8,128)(2,1)S(1)} collective-permute-done((bf16[256,2560]{1,0:T(8,128)(2,1)S(1)}, bf16[256,2560]{1,0:T(8,128)(2,1)S(1)}, u32[]{:S(2)}, u32[]{:S(2)}) %collective-permute-start.2) | collective-permute-done | bytes 1310752 | tf_op jit(solution)/shard_map/ppermute | solution.py:573
  36.0 0.0 copy-start.9
  36.1 2.1 %copy-done.9 = bf16[384,5120]{1,0:T(8,128)(2,1)S(1)} copy-done((bf16[384,5120]{1,0:T(8,128)(2,1)S(1)}, bf16[384,5120]{1,0:T(8,128)(2,1)}, u32[]{:S(2)}) %copy-start.9) | copy-done | bytes 3932184
  38.2 12.2 %project.1 = (bf16[384,512]{1,0:T(8,128)(2,1)S(1)}, bf16[384,1024]{1,0:T(8,128)(2,1)S(1)}) custom-call(bf16[384,5120]{1,0:T(8,128)(2,1)S(1)} %copy-done.9, f32[1,5120]{1,0:T(1,128)S(1)} %bitcast.27, f32[1,5120]{1,0:T(1,128)S(1)} %bitcast.28, bf16[2,5120,512]{2,1,0:T(8,128)(2,1)} %wqk_ref.1, bf16[5120,512]{1,0:T(8,128)(2,1)} %wv_ref.1, ...), custom_call_target="tpu_custom_call" | custom-call | flops 6039797760 | bytes 19660800 | tf_op jit(solution)/shard_map/project/pallas_call | solution.py:123
  50.4 0.6 collective-permute-start
  50.9 1.9 %collective-permute-done.there_ref = bf16[384,1024]{1,0:T(8,128)(2,1)S(1)} collective-permute-done((bf16[384,1024]{1,0:T(8,128)(2,1)S(1)}, bf16[384,1024]{1,0:T(8,128)(2,1)S(1)}, u32[]{:S(2)}, u32[]{:S(2)}) %collective-permute-start) | collective-permute-done | bytes 786464 | tf_op jit(solution)/shard_map/ppermute | solution.py:577
  52.9 3.8 %attend.1 = (bf16[384,512]{1,0:T(8,128)(2,1)S(1)}, bf16[208,512]{1,0:T(8,128)(2,1)S(1)}, bf16[112,512]{1,0:T(8,128)(2,1)S(1)}, bf16[112,512]{1,0:T(8,128)(2,1)S(1)}, bf16[112,512]{1,0:T(8,128)(2,1)S(1)}) custom-call(s32[3]{0:T(128)S(1)} %pad_add_fusion.at_ref, bf16[384,512]{1,0:T(8,128)(2,1)S(1)} %get-tuple-element.21.q_ref.refs_0_, ...), custom_call_target="tpu_custom_call" | custom-call | flops 603979776 | bytes 1572864 | tf_op jit(solution)/shard_map/attend/pallas_call | solution.py:199
  56.7 1.8 %collective-permute-start.1 = (bf16[384,512]{1,0:T(8,128)(2,1)S(1)}, bf16[384,512]{1,0:T(8,128)(2,1)S(1)}, u32[]{:S(2)}, u32[]{:S(2)}) collective-permute-start(bf16[384,512]{1,0:T(8,128)(2,1)S(1)} %get-tuple-element.23.near_ref), channel_id=1, source_target_pairs={{0,2},{2,0},{4,6},{6,4},{8,10},{10,8},{12,14},{14,12},{1,3},{3,1},... | collective-permute-start | bytes 1179656 | tf_op jit(solution)/shard_map/ppermute | solution.py:591
  58.5 1.6 collective-permute-start.7
  60.1 8.1 %collective-permute-done.1.far_ref = bf16[384,512]{1,0:T(8,128)(2,1)S(1)} collective-permute-done((bf16[384,512]{1,0:T(8,128)(2,1)S(1)}, bf16[384,512]{1,0:T(8,128)(2,1)S(1)}, u32[]{:S(2)}, u32[]{:S(2)}) %collective-permute-start.1) | collective-permute-done | bytes 393248 | tf_op jit(solution)/shard_map/ppermute | solution.py:591
  68.2 4.8 %project_out.1 = (bf16[384,640]{1,0:T(8,128)(2,1)S(1)}, f32[384,640]{1,0:T(8,128)S(1)}, f32[384,640]{1,0:T(8,128)S(1)}, f32[384,640]{1,0:T(8,128)S(1)}) custom-call(s32[3]{0:T(128)S(1)} %pad_add_fusion.at_ref, bf16[384,512]{1,0:T(8,128)(2,1)S(1)} %get-tuple-element.23.near_ref, bf16[384,512]{1,0:T(8,128)(2,1)S(1)} %collective-permute-done.1.far_ref, ...), custom_call_target="tpu_custom_call" | custom-call | flops 2013265920 | bytes 9175040 | tf_op jit(solution)/shard_map/project_out/pallas_call | solution.py:283
  73.0 0.0 copy-start.1
  73.0 0.0 copy-start.3
  73.0 0.0 copy-start.4
  73.0 0.0 copy-start.7
  73.1 0.0 copy-start.8
  73.1 1.8 %collective-permute-start.4 = (bf16[384,640]{1,0:T(8,128)(2,1)S(1)}, bf16[384,640]{1,0:T(8,128)(2,1)S(1)}, u32[]{:S(2)}, u32[]{:S(2)}) collective-permute-start(bf16[384,640]{1,0:T(8,128)(2,1)S(1)} %get-tuple-element.27), channel_id=1, source_target_pairs={{0,4},{2,6},{4,8},{6,10},{8,12},{10,14},{12,0},{14,2},{1,5},{3,7},... | collective-permute-start | bytes 1474568 | tf_op jit(solution)/shard_map/ppermute | solution.py:622
  74.9 1.6 collective-permute-start.10
  76.5 1.6 collective-permute-start.8
  78.1 1.2 collective-permute-start.11
  79.3 20.7 %collective-permute-done.8.refs_3_ = bf16[112,512]{1,0:T(8,128)(2,1)S(1)} collective-permute-done((bf16[112,512]{1,0:T(8,128)(2,1)S(1)}, bf16[112,512]{1,0:T(8,128)(2,1)S(1)}, u32[]{:S(2)}, u32[]{:S(2)}) %collective-permute-start.8) | collective-permute-done | bytes 114720 | tf_op jit(solution)/shard_map/ppermute | solution.py:587
  100.0 1.0 collective-permute-start.14
  101.0 2.7 %collective-permute-done.11.refs_1_ = bf16[112,512]{1,0:T(8,128)(2,1)S(1)} collective-permute-done((bf16[112,512]{1,0:T(8,128)(2,1)S(1)}, bf16[112,512]{1,0:T(8,128)(2,1)S(1)}, u32[]{:S(2)}, u32[]{:S(2)}) %collective-permute-start.11) | collective-permute-done | bytes 114720 | tf_op jit(solution)/shard_map/ppermute | solution.py:587
  103.7 1.7 %pair_maps.4 = (bf16[2,384,384]{2,1,0:T(8,128)(2,1)S(1)}, bf16[2,384,384]{2,1,0:T(8,128)(2,1)S(1)}) custom-call(s32[3]{0:T(128)S(1)} %pad_add_fusion.at_ref, bf16[384,512]{1,0:T(8,128)(2,1)S(1)} %get-tuple-element.21.q_ref.refs_0_, bf16[208,512]{1,0:T(8,128)(2,1)S(1)} %get-tuple-element.28.refs_1_, bf16[384,512]{1,0:T(8,128)(2,1)S(1)} %collective-permute-done.7.refs_2_, ...), custom_call_target="tpu_custom_call" | custom-call | flops 603979776 | bytes 2359296 | tf_op jit(solution)/shard_map/pair_maps/pallas_call | solution.py:347
  105.4 1.6 collective-permute-start.16
  107.0 0.1 collective-permute-start.19
  107.1 1.4 collective-permute-start.13
  108.5 1.3 pair_maps.5
  109.8 0.6 collective-permute-start.17
  110.4 0.1 add_convert_fusion.1
  110.5 4.8 %collective-permute-done.19.refs_0_ = bf16[128,512]{1,0:T(8,128)(2,1)S(1)} collective-permute-done((bf16[128,512]{1,0:T(8,128)(2,1)S(1)}, bf16[128,512]{1,0:T(8,128)(2,1)S(1)}, u32[]{:S(2)}, u32[]{:S(2)}) %collective-permute-start.19) | collective-permute-done | bytes 131104 | tf_op jit(solution)/shard_map/ppermute | solution.py:583
  115.3 1.0 pair_maps.7
  116.3 0.6 collective-permute-start.20
  116.8 4.0 %collective-permute-done.13.refs_0_ = bf16[256,512]{1,0:T(8,128)(2,1)S(1)} collective-permute-done((bf16[256,512]{1,0:T(8,128)(2,1)S(1)}, bf16[256,512]{1,0:T(8,128)(2,1)S(1)}, u32[]{:S(2)}, u32[]{:S(2)}) %collective-permute-start.13) | collective-permute-done | bytes 262176 | tf_op jit(solution)/shard_map/ppermute | solution.py:583
  120.9 1.1 pair_maps.6
  121.9 0.6 collective-permute-start.18
  122.5 7.6 %collective-permute-done.20.refs_5_ = bf16[1,128,384]{2,1,0:T(8,128)(2,1)S(1)} collective-permute-done((bf16[1,128,384]{2,1,0:T(8,128)(2,1)S(1)}, bf16[1,128,384]{2,1,0:T(8,128)(2,1)S(1)}, u32[]{:S(2)}, u32[]{:S(2)}) %collective-permute-start.20) | collective-permute-done | bytes 98336 | tf_op jit(solution)/shard_map/ppermute | solution.py:603
  130.2 11.3 %pair_block.3.refs_14_ = bf16[384,96,128]{2,1,0:T(8,128)(2,1)} custom-call(s32[3]{0:T(128)S(1)} %pad_add_fusion.at_ref, bf16[2,384,384]{2,1,0:T(8,128)(2,1)S(1)} %get-tuple-element.30.refs_0_, bf16[1,384,384]{2,1,0:T(8,128)(2,1)S(1)} %get-tuple-element.32.refs_1_, bf16[1,128,384]{2,1,0:T(8,128)(2,1)S(1)} %get-tuple-element.38.refs_2_, ...), custom_call_target="tpu_custom_call" | custom-call | flops 3221225472 | bytes 6291456 | tf_op jit(solution)/shard_map/pair_block/pallas_call | solution.py:487
  141.5 0.1 add_convert_fusion
  141.6 0.3 collective-permute-start.6
  141.9 11.3 %pair_block.4.refs_14_ = bf16[384,96,128]{2,1,0:T(8,128)(2,1)} custom-call(s32[3]{0:T(128)S(1)} %pad_add_fusion.at_ref, bf16[2,384,384]{2,1,0:T(8,128)(2,1)S(1)} %get-tuple-element.30.refs_0_, bf16[1,384,384]{2,1,0:T(8,128)(2,1)S(1)} %get-tuple-element.32.refs_1_, ...), custom_call_target="tpu_custom_call", output_to_operand_aliasing={{}: (15, {})} | custom-call | flops 3221225472 | bytes 6291456 | tf_op jit(solution)/shard_map/pair_block/pallas_call | solution.py:487
  153.3 11.3 %pair_block.5 = bf16[384,96,128]{2,1,0:T(8,128)(2,1)} custom-call(s32[3]{0:T(128)S(1)} %pad_add_fusion.at_ref, bf16[2,384,384]{2,1,0:T(8,128)(2,1)S(1)} %get-tuple-element.30.refs_0_, bf16[1,384,384]{2,1,0:T(8,128)(2,1)S(1)} %get-tuple-element.32.refs_1_, bf16[1,256,384]{2,1,0:T(8,128)(2,1)S(1)} %get-tuple-element.34.refs_2_, ...), custom_call_target="tpu_custom_call", output_to_operand_aliasing={{}: (15, {})} | custom-call | flops 3221225472 | bytes 6291456 | tf_op jit(solution)/shard_map/pair_block/pallas_call | solution.py:487
  164.5 1.1 convert_add_fusion
  (43 shorter events, 0.1 us)
Async XLA Ops:
  0.6 35.4 %copy-start.10 = (f32[5120]{0:T(1024)S(1)}, f32[5120]{0:T(1024)}, u32[]{:S(2)}) copy-start(f32[5120]{0:T(1024)} %param.15) | copy-start | bytes 61444
  0.6 35.4 %copy-start.11 = (f32[5120]{0:T(1024)S(1)}, f32[5120]{0:T(1024)}, u32[]{:S(2)}) copy-start(f32[5120]{0:T(1024)} %param.16) | copy-start | bytes 61444
  0.7 2.5 %copy-start = (bf16[512,5120]{1,0:T(8,128)(2,1)S(1)}, bf16[512,5120]{1,0:T(8,128)(2,1)}, u32[]{:S(2)}) copy-start(bf16[512,5120]{1,0:T(8,128)(2,1)} %w_ref.3) | copy-start | bytes 15728644
  4.2 31.8 %collective-permute-start.2 = (bf16[256,2560]{1,0:T(8,128)(2,1)S(1)}, bf16[256,2560]{1,0:T(8,128)(2,1)S(1)}, u32[]{:S(2)}, u32[]{:S(2)}) collective-permute-start(bf16[256,2560]{1,0:T(8,128)(2,1)S(1)} %pack_columns.1), channel_id=1, source_target_pairs={{0,2},{2,0},{4,6},{6,4},{8,10},{10,8},{12,14},{14,12},{1,3},{3,1},... | collective-permute-start | bytes 3932168 | tf_op jit(solution)/shard_map/ppermute | solution.py:573
  7.3 60.9 %slice-start = ((s8[5242880]{0:T(1024)(128)(4,1)}), s8[4194304]{0:T(1024)(128)(4,1)S(1)}, s32[]{:S(2)}) async-start(s8[5242880]{0:T(1024)(128)(4,1)} %bitcast.10), calls=%async_computation | async-start | bytes 8388608
  36.0 32.1 %collective-permute-start.3 = (bf16[256,2560]{1,0:T(8,128)(2,1)S(1)}, bf16[256,2560]{1,0:T(8,128)(2,1)S(1)}, u32[]{:S(2)}, u32[]{:S(2)}) collective-permute-start(bf16[256,2560]{1,0:T(8,128)(2,1)S(1)} %collective-permute-done.2.w_same_ref), channel_id=1, source_target_pairs={{0,1},{1,0},{2,3},{3,2},{4,5},{5,4},{6,7},{7,6},{8,9},{9,8},{10,11... | collective-permute-start | bytes 3932168 | tf_op jit(solution)/shard_map/ppermute | solution.py:592
  36.0 2.1 %copy-start.9 = (bf16[384,5120]{1,0:T(8,128)(2,1)S(1)}, bf16[384,5120]{1,0:T(8,128)(2,1)}, u32[]{:S(2)}) copy-start(bf16[384,5120]{1,0:T(8,128)(2,1)} %x_ref.1) | copy-start | bytes 11796484
  38.2 30.0 %slice-start.1 = ((s8[5242880]{0:T(1024)(128)(4,1)}), s8[1048576]{0:T(1024)(128)(4,1)S(1)}, s32[]{:S(2)}) async-start(s8[5242880]{0:T(1024)(128)(4,1)} %bitcast.10), calls=%async_computation.1 | async-start | bytes 2097152
  50.4 2.5 %collective-permute-start = (bf16[384,1024]{1,0:T(8,128)(2,1)S(1)}, bf16[384,1024]{1,0:T(8,128)(2,1)S(1)}, u32[]{:S(2)}, u32[]{:S(2)}) collective-permute-start(bf16[384,1024]{1,0:T(8,128)(2,1)S(1)} %get-tuple-element.22.own_ref), channel_id=1, source_target_pairs={{0,1},{1,0},{2,3},{3,2},{4,5},{5,4},{6,7},{7,6},{8,9},{9,8},{10,11... | collective-permute-start | bytes 2359304 | tf_op jit(solution)/shard_map/ppermute | solution.py:577
  56.7 11.5 %collective-permute-start.1 = (bf16[384,512]{1,0:T(8,128)(2,1)S(1)}, bf16[384,512]{1,0:T(8,128)(2,1)S(1)}, u32[]{:S(2)}, u32[]{:S(2)}) collective-permute-start(bf16[384,512]{1,0:T(8,128)(2,1)S(1)} %get-tuple-element.23.near_ref), channel_id=1, source_target_pairs={{0,2},{2,0},{4,6},{6,4},{8,10},{10,8},{12,14},{14,12},{1,3},{3,1},... | collective-permute-start | bytes 1179656 | tf_op jit(solution)/shard_map/ppermute | solution.py:591
  58.5 16.4 %collective-permute-start.7 = (bf16[384,512]{1,0:T(8,128)(2,1)S(1)}, bf16[384,512]{1,0:T(8,128)(2,1)S(1)}, u32[]{:S(2)}, u32[]{:S(2)}) collective-permute-start(bf16[384,512]{1,0:T(8,128)(2,1)S(1)} %get-tuple-element.21.q_ref.refs_0_), channel_id=1, source_target_pairs={{0,4},{2,6},{4,8},{6,10},{8,12},{10,14},{12,0},{14,2},{1,5},{3,7},... | collective-permute-start | bytes 1179656 | tf_op jit(solution)/shard_map/ppermute | solution.py:580
  73.0 57.2 %copy-start.1 = (bf16[128,512]{1,0:T(8,128)(2,1)S(1)}, bf16[128,512]{1,0:T(8,128)(2,1)}, u32[]{:S(2)}) copy-start(bf16[128,512]{1,0:T(8,128)(2,1)} %refs_10_.5) | copy-start | bytes 393220
  73.0 57.2 %copy-start.2 = (bf16[512,128]{1,0:T(8,128)(2,1)S(1)}, bf16[512,128]{1,0:T(8,128)(2,1)}, u32[]{:S(2)}) copy-start(bf16[512,128]{1,0:T(8,128)(2,1)} %refs_12_.5) | copy-start | bytes 393220
  73.0 57.2 %copy-start.3 = (bf16[32,128]{1,0:T(8,128)(2,1)S(1)}, bf16[32,128]{1,0:T(8,128)(2,1)}, u32[]{:S(2)}) copy-start(bf16[32,128]{1,0:T(8,128)(2,1)} %refs_6_.5) | copy-start | bytes 24580
  73.0 57.2 %copy-start.4 = (f32[512]{0:T(512)S(1)}, f32[512]{0:T(512)}, u32[]{:S(2)}) copy-start(f32[512]{0:T(512)} %param.25) | copy-start | bytes 6148
  73.0 57.2 %copy-start.5 = (f32[128]{0:T(128)S(1)}, f32[128]{0:T(128)}, u32[]{:S(2)}) copy-start(f32[128]{0:T(128)} %param.21) | copy-start | bytes 1540
  73.0 57.2 %copy-start.6 = (f32[128]{0:T(128)S(1)}, f32[128]{0:T(128)}, u32[]{:S(2)}) copy-start(f32[128]{0:T(128)} %param.22) | copy-start | bytes 1540
  73.0 57.2 %copy-start.7 = (f32[128]{0:T(128)S(1)}, f32[128]{0:T(128)}, u32[]{:S(2)}) copy-start(f32[128]{0:T(128)} %param.23) | copy-start | bytes 1540
  73.1 57.2 %copy-start.8 = (f32[128]{0:T(128)S(1)}, f32[128]{0:T(128)}, u32[]{:S(2)}) copy-start(f32[128]{0:T(128)} %param.27) | copy-start | bytes 1540
  73.1 36.7 %collective-permute-start.4 = (bf16[384,640]{1,0:T(8,128)(2,1)S(1)}, bf16[384,640]{1,0:T(8,128)(2,1)S(1)}, u32[]{:S(2)}, u32[]{:S(2)}) collective-permute-start(bf16[384,640]{1,0:T(8,128)(2,1)S(1)} %get-tuple-element.27), channel_id=1, source_target_pairs={{0,4},{2,6},{4,8},{6,10},{8,12},{10,14},{12,0},{14,2},{1,5},{3,7},... | collective-permute-start | bytes 1474568 | tf_op jit(solution)/shard_map/ppermute | solution.py:622
  74.9 32.1 %collective-permute-start.10 = (bf16[384,512]{1,0:T(8,128)(2,1)S(1)}, bf16[384,512]{1,0:T(8,128)(2,1)S(1)}, u32[]{:S(2)}, u32[]{:S(2)}) collective-permute-start(bf16[384,512]{1,0:T(8,128)(2,1)S(1)} %collective-permute-done.7.refs_2_), channel_id=1, source_target_pairs={{0,4},{2,6},{4,8},{6,10},{8,12},{10,14},{12,0},{14,2},{1,5},{3,7},... | collective-permute-start | bytes 1179656 | tf_op jit(solution)/shard_map/ppermute | solution.py:580
  76.5 23.5 %collective-permute-start.8 = (bf16[112,512]{1,0:T(8,128)(2,1)S(1)}, bf16[112,512]{1,0:T(8,128)(2,1)S(1)}, u32[]{:S(2)}, u32[]{:S(2)}) collective-permute-start(bf16[112,512]{1,0:T(8,128)(2,1)S(1)} %get-tuple-element.29), channel_id=1, source_target_pairs={{0,4},{2,6},{4,8},{6,10},{8,12},{10,14},{12,0},{14,2},{1,5},{3,7},... | collective-permute-start | bytes 344072 | tf_op jit(solution)/shard_map/ppermute | solution.py:587
  78.1 25.6 %collective-permute-start.11 = (bf16[112,512]{1,0:T(8,128)(2,1)S(1)}, bf16[112,512]{1,0:T(8,128)(2,1)S(1)}, u32[]{:S(2)}, u32[]{:S(2)}) collective-permute-start(bf16[112,512]{1,0:T(8,128)(2,1)S(1)} %get-tuple-element.31), channel_id=1, source_target_pairs={{0,8},{2,10},{4,12},{6,14},{8,0},{10,2},{12,4},{14,6},{1,9},{3,11}... | collective-permute-start | bytes 344072 | tf_op jit(solution)/shard_map/ppermute | solution.py:587
  100.0 3.7 %collective-permute-start.9 = (bf16[112,512]{1,0:T(8,128)(2,1)S(1)}, bf16[112,512]{1,0:T(8,128)(2,1)S(1)}, u32[]{:S(2)}, u32[]{:S(2)}) collective-permute-start(bf16[112,512]{1,0:T(8,128)(2,1)S(1)} %collective-permute-done.8.refs_3_), channel_id=1, source_target_pairs={{0,1},{1,0},{2,3},{3,2},{4,5},{5,4},{6,7},{7,6},{8,9},{9,8},{10,11... | collective-permute-start | bytes 344072 | tf_op jit(solution)/shard_map/ppermute | solution.py:588
  100.0 7.1 %collective-permute-start.14 = (bf16[112,512]{1,0:T(8,128)(2,1)S(1)}, bf16[112,512]{1,0:T(8,128)(2,1)S(1)}, u32[]{:S(2)}, u32[]{:S(2)}) collective-permute-start(bf16[112,512]{1,0:T(8,128)(2,1)S(1)} %get-tuple-element.33), channel_id=1, source_target_pairs={{0,12},{2,14},{4,0},{6,2},{8,4},{10,6},{12,8},{14,10},{1,13},{3,15... | collective-permute-start | bytes 344072 | tf_op jit(solution)/shard_map/ppermute | solution.py:587
  103.7 4.8 %collective-permute-start.12 = (bf16[112,512]{1,0:T(8,128)(2,1)S(1)}, bf16[112,512]{1,0:T(8,128)(2,1)S(1)}, u32[]{:S(2)}, u32[]{:S(2)}) collective-permute-start(bf16[112,512]{1,0:T(8,128)(2,1)S(1)} %collective-permute-done.11.refs_1_), channel_id=1, source_target_pairs={{0,1},{1,0},{2,3},{3,2},{4,5},{5,4},{6,7},{7,6},{8,9},{9,8},{10,11... | collective-permute-start | bytes 344072 | tf_op jit(solution)/shard_map/ppermute | solution.py:588
  105.4 24.7 %collective-permute-start.16 = (bf16[2,384,384]{2,1,0:T(8,128)(2,1)S(1)}, bf16[2,384,384]{2,1,0:T(8,128)(2,1)S(1)}, u32[]{:S(2)}, u32[]{:S(2)}) collective-permute-start(bf16[2,384,384]{2,1,0:T(8,128)(2,1)S(1)} %get-tuple-element.35), channel_id=1, source_target_pairs={{0,2},{2,0},{4,6},{6,4},{8,10},{10,8},{12,14},{14,12},{1,3},{3,1},... | collective-permute-start | bytes 1769480 | tf_op jit(solution)/shard_map/ppermute | solution.py:603
  107.0 8.2 %collective-permute-start.19 = (bf16[128,512]{1,0:T(8,128)(2,1)S(1)}, bf16[128,512]{1,0:T(8,128)(2,1)S(1)}, u32[]{:S(2)}, u32[]{:S(2)}) collective-permute-start(bf16[128,512]{1,0:T(8,128)(2,1)S(1)} %slice.9), channel_id=1, source_target_pairs={{0,4},{2,6},{4,8},{6,10},{8,12},{10,14},{12,0},{14,2},{1,5},{3,7},... | collective-permute-start | bytes 393224 | tf_op jit(solution)/shard_map/ppermute | solution.py:583
  107.1 13.7 %collective-permute-start.13 = (bf16[256,512]{1,0:T(8,128)(2,1)S(1)}, bf16[256,512]{1,0:T(8,128)(2,1)S(1)}, u32[]{:S(2)}, u32[]{:S(2)}) collective-permute-start(bf16[256,512]{1,0:T(8,128)(2,1)S(1)} %slice.8), channel_id=1, source_target_pairs={{0,4},{2,6},{4,8},{6,10},{8,12},{10,14},{12,0},{14,2},{1,5},{3,7},... | collective-permute-start | bytes 786440 | tf_op jit(solution)/shard_map/ppermute | solution.py:583
  108.5 6.8 %collective-permute-start.15 = (bf16[112,512]{1,0:T(8,128)(2,1)S(1)}, bf16[112,512]{1,0:T(8,128)(2,1)S(1)}, u32[]{:S(2)}, u32[]{:S(2)}) collective-permute-start(bf16[112,512]{1,0:T(8,128)(2,1)S(1)} %collective-permute-done.14.refs_1_), channel_id=1, source_target_pairs={{0,1},{1,0},{2,3},{3,2},{4,5},{5,4},{6,7},{7,6},{8,9},{9,8},{10,11... | collective-permute-start | bytes 344072 | tf_op jit(solution)/shard_map/ppermute | solution.py:588
  109.8 20.4 %collective-permute-start.17 = (bf16[1,384,384]{2,1,0:T(8,128)(2,1)S(1)}, bf16[1,384,384]{2,1,0:T(8,128)(2,1)S(1)}, u32[]{:S(2)}, u32[]{:S(2)}) collective-permute-start(bf16[1,384,384]{2,1,0:T(8,128)(2,1)S(1)} %get-tuple-element.36), channel_id=1, source_target_pairs={{0,2},{2,0},{4,6},{6,4},{8,10},{10,8},{12,14},{14,12},{1,3},{3,1},... | collective-permute-start | bytes 884744 | tf_op jit(solution)/shard_map/ppermute | solution.py:603
  115.3 26.3 %collective-permute-start.5 = (bf16[384,640]{1,0:T(8,128)(2,1)S(1)}, bf16[384,640]{1,0:T(8,128)(2,1)S(1)}, u32[]{:S(2)}, u32[]{:S(2)}) collective-permute-start(bf16[384,640]{1,0:T(8,128)(2,1)S(1)} %add_convert_fusion.1), channel_id=1, source_target_pairs={{0,4},{2,6},{4,8},{6,10},{8,12},{10,14},{12,0},{14,2},{1,5},{3,7},... | collective-permute-start | bytes 1474568 | tf_op jit(solution)/shard_map/ppermute | solution.py:622
  116.3 13.9 %collective-permute-start.20 = (bf16[1,128,384]{2,1,0:T(8,128)(2,1)S(1)}, bf16[1,128,384]{2,1,0:T(8,128)(2,1)S(1)}, u32[]{:S(2)}, u32[]{:S(2)}) collective-permute-start(bf16[1,128,384]{2,1,0:T(8,128)(2,1)S(1)} %get-tuple-element.39), channel_id=1, source_target_pairs={{0,2},{2,0},{4,6},{6,4},{8,10},{10,8},{12,14},{14,12},{1,3},{3,1},... | collective-permute-start | bytes 294920 | tf_op jit(solution)/shard_map/ppermute | solution.py:603
  121.9 20.0 %collective-permute-start.18 = (bf16[1,256,384]{2,1,0:T(8,128)(2,1)S(1)}, bf16[1,256,384]{2,1,0:T(8,128)(2,1)S(1)}, u32[]{:S(2)}, u32[]{:S(2)}) collective-permute-start(bf16[1,256,384]{2,1,0:T(8,128)(2,1)S(1)} %get-tuple-element.37), channel_id=1, source_target_pairs={{0,2},{2,0},{4,6},{6,4},{8,10},{10,8},{12,14},{14,12},{1,3},{3,1},... | collective-permute-start | bytes 589832 | tf_op jit(solution)/shard_map/ppermute | solution.py:603
  141.6 22.9 %collective-permute-start.6 = (bf16[384,640]{1,0:T(8,128)(2,1)S(1)}, bf16[384,640]{1,0:T(8,128)(2,1)S(1)}, u32[]{:S(2)}, u32[]{:S(2)}) collective-permute-start(bf16[384,640]{1,0:T(8,128)(2,1)S(1)} %add_convert_fusion), channel_id=1, source_target_pairs={{0,4},{2,6},{4,8},{6,10},{8,12},{10,14},{12,0},{14,2},{1,5},{3,7},... | collective-permute-start | bytes 1474568 | tf_op jit(solution)/shard_map/ppermute | solution.py:622

commit v3 on v2

--- a/solution.py
+++ b/solution.py
@@ -29,6 +29,10 @@
 
 def sds(shape, dtype):
     return jax.ShapeDtypeStruct(shape, dtype)
+
+
+def chip_at(place):
+    return place + lax.div(place, 2) * (1 - 2 * lax.rem(place, 2))
 
 
 VMEM = pl.BlockSpec(memory_space=pltpu.VMEM)
@@ -184,11 +188,11 @@
         far = there_ref[start, 0:width].astype(F32)
         return (near * mine + far * (1.0 - mine)).astype(BF16)
 
-    local_ref[0:columns, :] = key_rows(z, y)
-    local_ref[columns : 2 * columns, :] = key_rows(z, 1 - y)
+    local_ref[0:columns, :] = key_rows(chip_at(z), y)
+    local_ref[columns : 2 * columns, :] = key_rows(chip_at(z), 1 - y)
     local_ref[2 * columns : 2 * columns + 16, :] = level_ref[...]
     for distance, share_ref in enumerate(share_refs, 1):
-        chip = lax.rem(z + distance, ring)
+        chip = chip_at(lax.rem(z + distance, ring))
         share_ref[0:columns, :] = key_rows(chip, core)
         share_ref[columns : columns + 16, :] = level_ref[...]
 
@@ -216,7 +220,7 @@
     copies = []
     piece = depth // sems.shape[1]
     for n in range(count):
-        block = 2 * lax.rem(z + (2 * count - 1 - n), count) + 1 - y
+        block = 2 * chip_at(lax.rem(z + (2 * count - 1 - n), count)) + 1 - y
         for part in range(sems.shape[1]):
             copies.append(
                 pltpu.make_async_copy(
@@ -256,7 +260,7 @@
     core, z, y = at_ref[0], at_ref[1], at_ref[2]
     copies = []
     for n in range(count):
-        block = 2 * lax.rem(z + (2 * count - 1 - n), count) + y
+        block = 2 * chip_at(lax.rem(z + (2 * count - 1 - n), count)) + y
         copies.append(
             pltpu.make_async_copy(
                 w_ref.at[:, pl.ds(pl.multiple_of(block * tile, tile), tile)], w.at[n], sems.at[n]
@@ -377,7 +381,7 @@
         column = lax.broadcasted_iota(jnp.int32, (heads_all, heads_all), 1)
         ring = count // 2
         distance = lax.rem(row // heads, ring)
-        chip = lax.rem(at_ref[1] + ring - distance, ring)
+        chip = chip_at(lax.rem(at_ref[1] + ring - distance, ring))
         side = jnp.where(row // heads >= ring, 1 - at_ref[2], at_ref[2])
         head = (2 * chip + side) * heads + lax.rem(row, heads)
         sort = jnp.where(column == head, 1.0, 0.0).astype(BF16)
@@ -561,13 +565,16 @@
     swap_y = [(m, m ^ 1) for m in range(parts)]
 
     def rotate_z(by):
-        return [(2 * a + b, 2 * ((a + by) % ring) + b) for a in range(ring) for b in range(2)]
+        chips = [a ^ (a >> 1) for a in range(ring)]
+        return [
+            (2 * chips[a] + b, 2 * chips[(a + by) % ring] + b) for a in range(ring) for b in range(2)
+        ]
 
     half = HD // 2
     freqs = 10000.0 ** (-jnp.arange(half, dtype=F32) / half)
     positions = core * rows + jnp.arange(rows, dtype=jnp.int32)
     angles = positions.astype(F32)[:, None] * freqs[None, :]
-    at = jnp.stack([core, z, y]).astype(jnp.int32)
+    at = jnp.stack([core, chip_at(z), y]).astype(jnp.int32)
 
     w_half = pack_columns(at, w_out, ring)
     w_same = lax.ppermute(w_half, "mp", swap_y)

time: 166 us -> 168 us (1.012)
  starting transfers between devices: 19.2 us -> 28.1 us
  waiting for transfers between devices: 77.8 us -> 71.2 us
    ppermute x3, starting transfers between devices: 2.13 us -> 6.68 us  [per_device_fast(): total = tail + lax.ppermute(sent, 'mp', rotate_z(1)).astype(F32)]
    ppermute x2, starting transfers between devices: 1.42 us -> 5.5 us  [per_device_fast(): lax.ppermute(part, 'mp', rotate_z(1))]
    ppermute x4, waiting for transfers between devices: 7.62 us -> 5.11 us  [per_device_fast(): other_maps.append((lax.ppermute(other_side, 'mp', swap_y), start))]
    ppermute x2, waiting for transfers between devices: 8.8 us -> 6.39 us  [per_device_fast(): lax.ppermute(part, 'mp', rotate_z(1))]
    ppermute x3, waiting for transfers between devices: 23.4 us -> 21.7 us  [per_device_fast(): mine = lax.ppermute(shares[d - 1], 'mp', rotate_z(d))]
  transfers between devices with their start and end apart: 21 -> 21, of which waited for: 8 -> 9; matrix products, arithmetic and copies ran while one was open for 1% -> 1% of each run, Pallas kernels for 36% -> 36%
where the time goes in v3:
time: 168 us
  waiting for transfers between devices  71.2 us (42%)
  Pallas kernels  60.7 us (36%)
  starting transfers between devices  28.1 us (17%)
  local copies, waits for them, and re-layouts  4.69 us (3%)
  other arithmetic  2.13 us (1%)
    pallas_call x3, Pallas kernels, pair_block_fast(): pl.pallas_call(functools.partial(pair_kernel, factor, len(maps), count, l...  33.9 us
    ppermute x1, waiting for transfers between devices, per_device_fast(): w_same = lax.ppermute(w_half, 'mp', swap_y)  28 us
    ppermute x3, waiting for transfers between devices, per_device_fast(): mine = lax.ppermute(shares[d - 1], 'mp', rotate_z(d))  21.7 us
    pallas_call x1, Pallas kernels, project(): pl.pallas_call(project_kernel, in_specs=[HBM, VMEM, VMEM, HBM, HBM, VMEM,...  12.2 us
    ppermute x1, waiting for transfers between devices, per_device_fast(): far = lax.ppermute(near, 'mp', swap_y)  8.09 us
    ppermute x3, starting transfers between devices, per_device_fast(): total = tail + lax.ppermute(sent, 'mp', rotate_z(1)).astype(F32)  6.68 us
    ppermute x2, waiting for transfers between devices, per_device_fast(): lax.ppermute(part, 'mp', rotate_z(1))  6.39 us
    ppermute x2, starting transfers between devices, per_device_fast(): lax.ppermute(part, 'mp', rotate_z(1))  5.5 us
  transfers between devices with their start and end apart: 21, of which 9 were waited for; matrix products, arithmetic and copies ran while one was open for 1% of the time, Pallas kernels for 36%

profile of v3, /device:TPU:0, one launch (start us, length us, event | category | flops | bytes accessed | tf_op | source)
XLA Modules:
  0.0 167.9 jit_solution(15882908172090097135)
XLA Ops:
  0.7 0.1 pad_add_fusion.at_ref
  0.8 2.5 %copy-done = bf16[512,5120]{1,0:T(8,128)(2,1)S(1)} copy-done((bf16[512,5120]{1,0:T(8,128)(2,1)S(1)}, bf16[512,5120]{1,0:T(8,128)(2,1)}, u32[]{:S(2)}) %copy-start) | copy-done | bytes 5242904
  3.2 1.0 pack_columns.1
  4.2 3.1 %collective-permute-start.2 = (bf16[256,2560]{1,0:T(8,128)(2,1)S(1)}, bf16[256,2560]{1,0:T(8,128)(2,1)S(1)}, u32[]{:S(2)}, u32[]{:S(2)}) collective-permute-start(bf16[256,2560]{1,0:T(8,128)(2,1)S(1)} %pack_columns.1), channel_id=1, source_target_pairs={{0,2},{2,0},{4,6},{6,4},{8,10},{10,8},{12,14},{14,12},{1,3},{3,1},... | collective-permute-start | bytes 3932168 | tf_op jit(solution)/shard_map/ppermute | solution.py:580
  7.3 0.8 multiply_sine_fusion
  8.1 28.0 %collective-permute-done.2.w_same_ref = bf16[256,2560]{1,0:T(8,128)(2,1)S(1)} collective-permute-done((bf16[256,2560]{1,0:T(8,128)(2,1)S(1)}, bf16[256,2560]{1,0:T(8,128)(2,1)S(1)}, u32[]{:S(2)}, u32[]{:S(2)}) %collective-permute-start.2) | collective-permute-done | bytes 1310752 | tf_op jit(solution)/shard_map/ppermute | solution.py:580
  36.1 2.1 %copy-done.9 = bf16[384,5120]{1,0:T(8,128)(2,1)S(1)} copy-done((bf16[384,5120]{1,0:T(8,128)(2,1)S(1)}, bf16[384,5120]{1,0:T(8,128)(2,1)}, u32[]{:S(2)}) %copy-start.9) | copy-done | bytes 3932184
  38.2 12.2 %project.1 = (bf16[384,512]{1,0:T(8,128)(2,1)S(1)}, bf16[384,1024]{1,0:T(8,128)(2,1)S(1)}) custom-call(bf16[384,5120]{1,0:T(8,128)(2,1)S(1)} %copy-done.9, f32[1,5120]{1,0:T(1,128)S(1)} %bitcast.27, f32[1,5120]{1,0:T(1,128)S(1)} %bitcast.28, bf16[2,5120,512]{2,1,0:T(8,128)(2,1)} %wqk_ref.1, bf16[5120,512]{1,0:T(8,128)(2,1)} %wv_ref.1, ...), custom_call_target="tpu_custom_call" | custom-call | flops 6039797760 | bytes 19660800 | tf_op jit(solution)/shard_map/project/pallas_call | solution.py:127
  50.4 0.6 collective-permute-start
  51.0 1.9 %collective-permute-done.there_ref = bf16[384,1024]{1,0:T(8,128)(2,1)S(1)} collective-permute-done((bf16[384,1024]{1,0:T(8,128)(2,1)S(1)}, bf16[384,1024]{1,0:T(8,128)(2,1)S(1)}, u32[]{:S(2)}, u32[]{:S(2)}) %collective-permute-start) | collective-permute-done | bytes 786464 | tf_op jit(solution)/shard_map/ppermute | solution.py:584
  52.9 3.8 %attend.1 = (bf16[384,512]{1,0:T(8,128)(2,1)S(1)}, bf16[208,512]{1,0:T(8,128)(2,1)S(1)}, bf16[112,512]{1,0:T(8,128)(2,1)S(1)}, bf16[112,512]{1,0:T(8,128)(2,1)S(1)}, bf16[112,512]{1,0:T(8,128)(2,1)S(1)}) custom-call(s32[3]{0:T(128)S(1)} %pad_add_fusion.at_ref, bf16[384,512]{1,0:T(8,128)(2,1)S(1)} %get-tuple-element.21.q_ref.refs_0_, ...), custom_call_target="tpu_custom_call" | custom-call | flops 603979776 | bytes 1572864 | tf_op jit(solution)/shard_map/attend/pallas_call | solution.py:203
  56.7 1.8 %collective-permute-start.1 = (bf16[384,512]{1,0:T(8,128)(2,1)S(1)}, bf16[384,512]{1,0:T(8,128)(2,1)S(1)}, u32[]{:S(2)}, u32[]{:S(2)}) collective-permute-start(bf16[384,512]{1,0:T(8,128)(2,1)S(1)} %get-tuple-element.23.near_ref), channel_id=1, source_target_pairs={{0,2},{2,0},{4,6},{6,4},{8,10},{10,8},{12,14},{14,12},{1,3},{3,1},... | collective-permute-start | bytes 1179656 | tf_op jit(solution)/shard_map/ppermute | solution.py:598
  58.5 1.6 collective-permute-start.7
  60.1 8.1 %collective-permute-done.1.far_ref = bf16[384,512]{1,0:T(8,128)(2,1)S(1)} collective-permute-done((bf16[384,512]{1,0:T(8,128)(2,1)S(1)}, bf16[384,512]{1,0:T(8,128)(2,1)S(1)}, u32[]{:S(2)}, u32[]{:S(2)}) %collective-permute-start.1) | collective-permute-done | bytes 393248 | tf_op jit(solution)/shard_map/ppermute | solution.py:598
  68.2 4.8 %project_out.1 = (bf16[384,640]{1,0:T(8,128)(2,1)S(1)}, f32[384,640]{1,0:T(8,128)S(1)}, f32[384,640]{1,0:T(8,128)S(1)}, f32[384,640]{1,0:T(8,128)S(1)}) custom-call(s32[3]{0:T(128)S(1)} %pad_add_fusion.at_ref, bf16[384,512]{1,0:T(8,128)(2,1)S(1)} %get-tuple-element.23.near_ref, bf16[384,512]{1,0:T(8,128)(2,1)S(1)} %collective-permute-done.1.far_ref, ...), custom_call_target="tpu_custom_call" | custom-call | flops 2013265920 | bytes 9175040 | tf_op jit(solution)/shard_map/project_out/pallas_call | solution.py:287
  73.0 0.0 copy-start.1
  73.0 0.0 copy-start.2
  73.1 0.0 copy-start.5
  73.1 0.0 copy-start.6
  73.1 1.8 %collective-permute-start.4 = (bf16[384,640]{1,0:T(8,128)(2,1)S(1)}, bf16[384,640]{1,0:T(8,128)(2,1)S(1)}, u32[]{:S(2)}, u32[]{:S(2)}) collective-permute-start(bf16[384,640]{1,0:T(8,128)(2,1)S(1)} %get-tuple-element.27), channel_id=1, source_target_pairs={{0,4},{2,6},{4,12},{6,14},{12,8},{14,10},{8,0},{10,2},{1,5},{3,7},... | collective-permute-start | bytes 1474568 | tf_op jit(solution)/shard_map/ppermute | solution.py:629
  75.0 2.6 %collective-permute-start.10 = (bf16[384,512]{1,0:T(8,128)(2,1)S(1)}, bf16[384,512]{1,0:T(8,128)(2,1)S(1)}, u32[]{:S(2)}, u32[]{:S(2)}) collective-permute-start(bf16[384,512]{1,0:T(8,128)(2,1)S(1)} %collective-permute-done.7.refs_2_), channel_id=1, source_target_pairs={{0,4},{2,6},{4,12},{6,14},{12,8},{14,10},{8,0},{10,2},{1,5},{3,7},... | collective-permute-start | bytes 1179656 | tf_op jit(solution)/shard_map/ppermute | solution.py:587
  77.5 0.5 collective-permute-start.8
  78.0 1.3 collective-permute-start.11
  79.3 20.9 %collective-permute-done.8.refs_3_ = bf16[112,512]{1,0:T(8,128)(2,1)S(1)} collective-permute-done((bf16[112,512]{1,0:T(8,128)(2,1)S(1)}, bf16[112,512]{1,0:T(8,128)(2,1)S(1)}, u32[]{:S(2)}, u32[]{:S(2)}) %collective-permute-start.8) | collective-permute-done | bytes 114720 | tf_op jit(solution)/shard_map/ppermute | solution.py:594
  100.2 0.5 collective-permute-start.14
  100.7 0.8 collective-permute-done.11.refs_1_
  101.5 0.1 collective-permute-done.9.refs_4_
  101.6 1.7 %pair_maps.4 = (bf16[2,384,384]{2,1,0:T(8,128)(2,1)S(1)}, bf16[2,384,384]{2,1,0:T(8,128)(2,1)S(1)}) custom-call(s32[3]{0:T(128)S(1)} %pad_add_fusion.at_ref, bf16[384,512]{1,0:T(8,128)(2,1)S(1)} %get-tuple-element.21.q_ref.refs_0_, bf16[208,512]{1,0:T(8,128)(2,1)S(1)} %get-tuple-element.28.refs_1_, bf16[384,512]{1,0:T(8,128)(2,1)S(1)} %collective-permute-done.7.refs_2_, ...), custom_call_target="tpu_custom_call" | custom-call | flops 603979776 | bytes 2359296 | tf_op jit(solution)/shard_map/pair_maps/pallas_call | solution.py:351
  103.3 1.6 collective-permute-start.16
  104.9 4.5 %collective-permute-start.19 = (bf16[128,512]{1,0:T(8,128)(2,1)S(1)}, bf16[128,512]{1,0:T(8,128)(2,1)S(1)}, u32[]{:S(2)}, u32[]{:S(2)}) collective-permute-start(bf16[128,512]{1,0:T(8,128)(2,1)S(1)} %slice.9), channel_id=1, source_target_pairs={{0,4},{2,6},{4,12},{6,14},{12,8},{14,10},{8,0},{10,2},{1,5},{3,7},... | collective-permute-start | bytes 393224 | tf_op jit(solution)/shard_map/ppermute | solution.py:590
  109.4 1.0 collective-permute-start.13
  110.5 1.2 pair_maps.5
  111.8 0.6 collective-permute-start.17
  112.3 0.1 add_convert_fusion.1
  112.5 3.2 %collective-permute-done.19.refs_0_ = bf16[128,512]{1,0:T(8,128)(2,1)S(1)} collective-permute-done((bf16[128,512]{1,0:T(8,128)(2,1)S(1)}, bf16[128,512]{1,0:T(8,128)(2,1)S(1)}, u32[]{:S(2)}, u32[]{:S(2)}) %collective-permute-start.19) | collective-permute-done | bytes 131104 | tf_op jit(solution)/shard_map/ppermute | solution.py:590
  115.7 0.1 collective-permute-start.5
  115.8 1.0 pair_maps.7
  116.8 1.3 collective-permute-start.20
  118.1 3.2 %collective-permute-done.13.refs_0_ = bf16[256,512]{1,0:T(8,128)(2,1)S(1)} collective-permute-done((bf16[256,512]{1,0:T(8,128)(2,1)S(1)}, bf16[256,512]{1,0:T(8,128)(2,1)S(1)}, u32[]{:S(2)}, u32[]{:S(2)}) %collective-permute-start.13) | collective-permute-done | bytes 262176 | tf_op jit(solution)/shard_map/ppermute | solution.py:590
  121.3 1.1 pair_maps.6
  122.3 0.6 collective-permute-start.18
  122.9 5.1 %collective-permute-done.20.refs_5_ = bf16[1,128,384]{2,1,0:T(8,128)(2,1)S(1)} collective-permute-done((bf16[1,128,384]{2,1,0:T(8,128)(2,1)S(1)}, bf16[1,128,384]{2,1,0:T(8,128)(2,1)S(1)}, u32[]{:S(2)}, u32[]{:S(2)}) %collective-permute-start.20) | collective-permute-done | bytes 98336 | tf_op jit(solution)/shard_map/ppermute | solution.py:610
  128.1 11.3 %pair_block.3.refs_14_ = bf16[384,96,128]{2,1,0:T(8,128)(2,1)} custom-call(s32[3]{0:T(128)S(1)} %pad_add_fusion.at_ref, bf16[2,384,384]{2,1,0:T(8,128)(2,1)S(1)} %get-tuple-element.30.refs_0_, bf16[1,384,384]{2,1,0:T(8,128)(2,1)S(1)} %get-tuple-element.32.refs_1_, bf16[1,128,384]{2,1,0:T(8,128)(2,1)S(1)} %get-tuple-element.38.refs_2_, ...), custom_call_target="tpu_custom_call" | custom-call | flops 3221225472 | bytes 6291456 | tf_op jit(solution)/shard_map/pair_block/pallas_call | solution.py:491
  139.4 0.1 add_convert_fusion
  139.5 4.7 %collective-permute-start.6 = (bf16[384,640]{1,0:T(8,128)(2,1)S(1)}, bf16[384,640]{1,0:T(8,128)(2,1)S(1)}, u32[]{:S(2)}, u32[]{:S(2)}) collective-permute-start(bf16[384,640]{1,0:T(8,128)(2,1)S(1)} %add_convert_fusion), channel_id=1, source_target_pairs={{0,4},{2,6},{4,12},{6,14},{12,8},{14,10},{8,0},{10,2},{1,5},{3,7},... | collective-permute-start | bytes 1474568 | tf_op jit(solution)/shard_map/ppermute | solution.py:629
  144.2 11.3 %pair_block.4.refs_14_ = bf16[384,96,128]{2,1,0:T(8,128)(2,1)} custom-call(s32[3]{0:T(128)S(1)} %pad_add_fusion.at_ref, bf16[2,384,384]{2,1,0:T(8,128)(2,1)S(1)} %get-tuple-element.30.refs_0_, bf16[1,384,384]{2,1,0:T(8,128)(2,1)S(1)} %get-tuple-element.32.refs_1_, ...), custom_call_target="tpu_custom_call", output_to_operand_aliasing={{}: (15, {})} | custom-call | flops 3221225472 | bytes 6291456 | tf_op jit(solution)/shard_map/pair_block/pallas_call | solution.py:491
  155.5 11.3 %pair_block.5 = bf16[384,96,128]{2,1,0:T(8,128)(2,1)} custom-call(s32[3]{0:T(128)S(1)} %pad_add_fusion.at_ref, bf16[2,384,384]{2,1,0:T(8,128)(2,1)S(1)} %get-tuple-element.30.refs_0_, bf16[1,384,384]{2,1,0:T(8,128)(2,1)S(1)} %get-tuple-element.32.refs_1_, bf16[1,256,384]{2,1,0:T(8,128)(2,1)S(1)} %get-tuple-element.34.refs_2_, ...), custom_call_target="tpu_custom_call", output_to_operand_aliasing={{}: (15, {})} | custom-call | flops 3221225472 | bytes 6291456 | tf_op jit(solution)/shard_map/pair_block/pallas_call | solution.py:491
  166.8 1.1 convert_add_fusion
  (43 shorter events, 0.1 us)
Async XLA Ops:
  0.6 35.4 %copy-start.10 = (f32[5120]{0:T(1024)S(1)}, f32[5120]{0:T(1024)}, u32[]{:S(2)}) copy-start(f32[5120]{0:T(1024)} %param.15) | copy-start | bytes 61444
  0.6 35.4 %copy-start.11 = (f32[5120]{0:T(1024)S(1)}, f32[5120]{0:T(1024)}, u32[]{:S(2)}) copy-start(f32[5120]{0:T(1024)} %param.16) | copy-start | bytes 61444
  0.8 2.5 %copy-start = (bf16[512,5120]{1,0:T(8,128)(2,1)S(1)}, bf16[512,5120]{1,0:T(8,128)(2,1)}, u32[]{:S(2)}) copy-start(bf16[512,5120]{1,0:T(8,128)(2,1)} %w_ref.3) | copy-start | bytes 15728644
  4.2 31.8 %collective-permute-start.2 = (bf16[256,2560]{1,0:T(8,128)(2,1)S(1)}, bf16[256,2560]{1,0:T(8,128)(2,1)S(1)}, u32[]{:S(2)}, u32[]{:S(2)}) collective-permute-start(bf16[256,2560]{1,0:T(8,128)(2,1)S(1)} %pack_columns.1), channel_id=1, source_target_pairs={{0,2},{2,0},{4,6},{6,4},{8,10},{10,8},{12,14},{14,12},{1,3},{3,1},... | collective-permute-start | bytes 3932168 | tf_op jit(solution)/shard_map/ppermute | solution.py:580
  7.3 60.9 %slice-start = ((s8[5242880]{0:T(1024)(128)(4,1)}), s8[4194304]{0:T(1024)(128)(4,1)S(1)}, s32[]{:S(2)}) async-start(s8[5242880]{0:T(1024)(128)(4,1)} %bitcast.10), calls=%async_computation | async-start | bytes 8388608
  36.1 32.1 %collective-permute-start.3 = (bf16[256,2560]{1,0:T(8,128)(2,1)S(1)}, bf16[256,2560]{1,0:T(8,128)(2,1)S(1)}, u32[]{:S(2)}, u32[]{:S(2)}) collective-permute-start(bf16[256,2560]{1,0:T(8,128)(2,1)S(1)} %collective-permute-done.2.w_same_ref), channel_id=1, source_target_pairs={{0,1},{1,0},{2,3},{3,2},{4,5},{5,4},{6,7},{7,6},{8,9},{9,8},{10,11... | collective-permute-start | bytes 3932168 | tf_op jit(solution)/shard_map/ppermute | solution.py:599
  36.1 2.1 %copy-start.9 = (bf16[384,5120]{1,0:T(8,128)(2,1)S(1)}, bf16[384,5120]{1,0:T(8,128)(2,1)}, u32[]{:S(2)}) copy-start(bf16[384,5120]{1,0:T(8,128)(2,1)} %x_ref.1) | copy-start | bytes 11796484
  38.2 30.0 %slice-start.1 = ((s8[5242880]{0:T(1024)(128)(4,1)}), s8[1048576]{0:T(1024)(128)(4,1)S(1)}, s32[]{:S(2)}) async-start(s8[5242880]{0:T(1024)(128)(4,1)} %bitcast.10), calls=%async_computation.1 | async-start | bytes 2097152
  50.4 2.5 %collective-permute-start = (bf16[384,1024]{1,0:T(8,128)(2,1)S(1)}, bf16[384,1024]{1,0:T(8,128)(2,1)S(1)}, u32[]{:S(2)}, u32[]{:S(2)}) collective-permute-start(bf16[384,1024]{1,0:T(8,128)(2,1)S(1)} %get-tuple-element.22.own_ref), channel_id=1, source_target_pairs={{0,1},{1,0},{2,3},{3,2},{4,5},{5,4},{6,7},{7,6},{8,9},{9,8},{10,11... | collective-permute-start | bytes 2359304 | tf_op jit(solution)/shard_map/ppermute | solution.py:584
  56.7 11.5 %collective-permute-start.1 = (bf16[384,512]{1,0:T(8,128)(2,1)S(1)}, bf16[384,512]{1,0:T(8,128)(2,1)S(1)}, u32[]{:S(2)}, u32[]{:S(2)}) collective-permute-start(bf16[384,512]{1,0:T(8,128)(2,1)S(1)} %get-tuple-element.23.near_ref), channel_id=1, source_target_pairs={{0,2},{2,0},{4,6},{6,4},{8,10},{10,8},{12,14},{14,12},{1,3},{3,1},... | collective-permute-start | bytes 1179656 | tf_op jit(solution)/shard_map/ppermute | solution.py:598
  58.5 16.4 %collective-permute-start.7 = (bf16[384,512]{1,0:T(8,128)(2,1)S(1)}, bf16[384,512]{1,0:T(8,128)(2,1)S(1)}, u32[]{:S(2)}, u32[]{:S(2)}) collective-permute-start(bf16[384,512]{1,0:T(8,128)(2,1)S(1)} %get-tuple-element.21.q_ref.refs_0_), channel_id=1, source_target_pairs={{0,4},{2,6},{4,12},{6,14},{12,8},{14,10},{8,0},{10,2},{1,5},{3,7},... | collective-permute-start | bytes 1179656 | tf_op jit(solution)/shard_map/ppermute | solution.py:587
  73.0 55.0 %copy-start.1 = (bf16[128,512]{1,0:T(8,128)(2,1)S(1)}, bf16[128,512]{1,0:T(8,128)(2,1)}, u32[]{:S(2)}) copy-start(bf16[128,512]{1,0:T(8,128)(2,1)} %refs_10_.5) | copy-start | bytes 393220
  73.0 55.0 %copy-start.2 = (bf16[512,128]{1,0:T(8,128)(2,1)S(1)}, bf16[512,128]{1,0:T(8,128)(2,1)}, u32[]{:S(2)}) copy-start(bf16[512,128]{1,0:T(8,128)(2,1)} %refs_12_.5) | copy-start | bytes 393220
  73.0 55.0 %copy-start.3 = (bf16[32,128]{1,0:T(8,128)(2,1)S(1)}, bf16[32,128]{1,0:T(8,128)(2,1)}, u32[]{:S(2)}) copy-start(bf16[32,128]{1,0:T(8,128)(2,1)} %refs_6_.5) | copy-start | bytes 24580
  73.1 55.0 %copy-start.4 = (f32[512]{0:T(512)S(1)}, f32[512]{0:T(512)}, u32[]{:S(2)}) copy-start(f32[512]{0:T(512)} %param.25) | copy-start | bytes 6148
  73.1 55.0 %copy-start.5 = (f32[128]{0:T(128)S(1)}, f32[128]{0:T(128)}, u32[]{:S(2)}) copy-start(f32[128]{0:T(128)} %param.21) | copy-start | bytes 1540
  73.1 55.0 %copy-start.6 = (f32[128]{0:T(128)S(1)}, f32[128]{0:T(128)}, u32[]{:S(2)}) copy-start(f32[128]{0:T(128)} %param.22) | copy-start | bytes 1540
  73.1 55.0 %copy-start.7 = (f32[128]{0:T(128)S(1)}, f32[128]{0:T(128)}, u32[]{:S(2)}) copy-start(f32[128]{0:T(128)} %param.23) | copy-start | bytes 1540
  73.1 55.0 %copy-start.8 = (f32[128]{0:T(128)S(1)}, f32[128]{0:T(128)}, u32[]{:S(2)}) copy-start(f32[128]{0:T(128)} %param.27) | copy-start | bytes 1540
  73.1 38.6 %collective-permute-start.4 = (bf16[384,640]{1,0:T(8,128)(2,1)S(1)}, bf16[384,640]{1,0:T(8,128)(2,1)S(1)}, u32[]{:S(2)}, u32[]{:S(2)}) collective-permute-start(bf16[384,640]{1,0:T(8,128)(2,1)S(1)} %get-tuple-element.27), channel_id=1, source_target_pairs={{0,4},{2,6},{4,12},{6,14},{12,8},{14,10},{8,0},{10,2},{1,5},{3,7},... | collective-permute-start | bytes 1474568 | tf_op jit(solution)/shard_map/ppermute | solution.py:629
  75.0 30.0 %collective-permute-start.10 = (bf16[384,512]{1,0:T(8,128)(2,1)S(1)}, bf16[384,512]{1,0:T(8,128)(2,1)S(1)}, u32[]{:S(2)}, u32[]{:S(2)}) collective-permute-start(bf16[384,512]{1,0:T(8,128)(2,1)S(1)} %collective-permute-done.7.refs_2_), channel_id=1, source_target_pairs={{0,4},{2,6},{4,12},{6,14},{12,8},{14,10},{8,0},{10,2},{1,5},{3,7},... | collective-permute-start | bytes 1179656 | tf_op jit(solution)/shard_map/ppermute | solution.py:587
  77.5 22.7 %collective-permute-start.8 = (bf16[112,512]{1,0:T(8,128)(2,1)S(1)}, bf16[112,512]{1,0:T(8,128)(2,1)S(1)}, u32[]{:S(2)}, u32[]{:S(2)}) collective-permute-start(bf16[112,512]{1,0:T(8,128)(2,1)S(1)} %get-tuple-element.29), channel_id=1, source_target_pairs={{0,4},{2,6},{4,12},{6,14},{12,8},{14,10},{8,0},{10,2},{1,5},{3,7},... | collective-permute-start | bytes 344072 | tf_op jit(solution)/shard_map/ppermute | solution.py:594
  78.0 23.5 %collective-permute-start.11 = (bf16[112,512]{1,0:T(8,128)(2,1)S(1)}, bf16[112,512]{1,0:T(8,128)(2,1)S(1)}, u32[]{:S(2)}, u32[]{:S(2)}) collective-permute-start(bf16[112,512]{1,0:T(8,128)(2,1)S(1)} %get-tuple-element.31), channel_id=1, source_target_pairs={{0,12},{2,14},{4,8},{6,10},{12,0},{14,2},{8,4},{10,6},{1,13},{3,15... | collective-permute-start | bytes 344072 | tf_op jit(solution)/shard_map/ppermute | solution.py:594
  100.2 1.3 collective-permute-start.9
  100.2 9.2 %collective-permute-start.14 = (bf16[112,512]{1,0:T(8,128)(2,1)S(1)}, bf16[112,512]{1,0:T(8,128)(2,1)S(1)}, u32[]{:S(2)}, u32[]{:S(2)}) collective-permute-start(bf16[112,512]{1,0:T(8,128)(2,1)S(1)} %get-tuple-element.33), channel_id=1, source_target_pairs={{0,8},{2,10},{4,0},{6,2},{12,4},{14,6},{8,12},{10,14},{1,9},{3,11}... | collective-permute-start | bytes 344072 | tf_op jit(solution)/shard_map/ppermute | solution.py:594
  101.5 9.0 %collective-permute-start.12 = (bf16[112,512]{1,0:T(8,128)(2,1)S(1)}, bf16[112,512]{1,0:T(8,128)(2,1)S(1)}, u32[]{:S(2)}, u32[]{:S(2)}) collective-permute-start(bf16[112,512]{1,0:T(8,128)(2,1)S(1)} %collective-permute-done.11.refs_1_), channel_id=1, source_target_pairs={{0,1},{1,0},{2,3},{3,2},{4,5},{5,4},{6,7},{7,6},{8,9},{9,8},{10,11... | collective-permute-start | bytes 344072 | tf_op jit(solution)/shard_map/ppermute | solution.py:595
  103.3 24.7 %collective-permute-start.16 = (bf16[2,384,384]{2,1,0:T(8,128)(2,1)S(1)}, bf16[2,384,384]{2,1,0:T(8,128)(2,1)S(1)}, u32[]{:S(2)}, u32[]{:S(2)}) collective-permute-start(bf16[2,384,384]{2,1,0:T(8,128)(2,1)S(1)} %get-tuple-element.35), channel_id=1, source_target_pairs={{0,2},{2,0},{4,6},{6,4},{8,10},{10,8},{12,14},{14,12},{1,3},{3,1},... | collective-permute-start | bytes 1769480 | tf_op jit(solution)/shard_map/ppermute | solution.py:610
  104.9 10.7 %collective-permute-start.19 = (bf16[128,512]{1,0:T(8,128)(2,1)S(1)}, bf16[128,512]{1,0:T(8,128)(2,1)S(1)}, u32[]{:S(2)}, u32[]{:S(2)}) collective-permute-start(bf16[128,512]{1,0:T(8,128)(2,1)S(1)} %slice.9), channel_id=1, source_target_pairs={{0,4},{2,6},{4,12},{6,14},{12,8},{14,10},{8,0},{10,2},{1,5},{3,7},... | collective-permute-start | bytes 393224 | tf_op jit(solution)/shard_map/ppermute | solution.py:590
  109.4 11.8 %collective-permute-start.13 = (bf16[256,512]{1,0:T(8,128)(2,1)S(1)}, bf16[256,512]{1,0:T(8,128)(2,1)S(1)}, u32[]{:S(2)}, u32[]{:S(2)}) collective-permute-start(bf16[256,512]{1,0:T(8,128)(2,1)S(1)} %slice.8), channel_id=1, source_target_pairs={{0,4},{2,6},{4,12},{6,14},{12,8},{14,10},{8,0},{10,2},{1,5},{3,7},... | collective-permute-start | bytes 786440 | tf_op jit(solution)/shard_map/ppermute | solution.py:590
  110.5 5.3 %collective-permute-start.15 = (bf16[112,512]{1,0:T(8,128)(2,1)S(1)}, bf16[112,512]{1,0:T(8,128)(2,1)S(1)}, u32[]{:S(2)}, u32[]{:S(2)}) collective-permute-start(bf16[112,512]{1,0:T(8,128)(2,1)S(1)} %collective-permute-done.14.refs_1_), channel_id=1, source_target_pairs={{0,1},{1,0},{2,3},{3,2},{4,5},{5,4},{6,7},{7,6},{8,9},{9,8},{10,11... | collective-permute-start | bytes 344072 | tf_op jit(solution)/shard_map/ppermute | solution.py:595
  111.8 16.2 %collective-permute-start.17 = (bf16[1,384,384]{2,1,0:T(8,128)(2,1)S(1)}, bf16[1,384,384]{2,1,0:T(8,128)(2,1)S(1)}, u32[]{:S(2)}, u32[]{:S(2)}) collective-permute-start(bf16[1,384,384]{2,1,0:T(8,128)(2,1)S(1)} %get-tuple-element.36), channel_id=1, source_target_pairs={{0,2},{2,0},{4,6},{6,4},{8,10},{10,8},{12,14},{14,12},{1,3},{3,1},... | collective-permute-start | bytes 884744 | tf_op jit(solution)/shard_map/ppermute | solution.py:610
  115.7 23.7 %collective-permute-start.5 = (bf16[384,640]{1,0:T(8,128)(2,1)S(1)}, bf16[384,640]{1,0:T(8,128)(2,1)S(1)}, u32[]{:S(2)}, u32[]{:S(2)}) collective-permute-start(bf16[384,640]{1,0:T(8,128)(2,1)S(1)} %add_convert_fusion.1), channel_id=1, source_target_pairs={{0,4},{2,6},{4,12},{6,14},{12,8},{14,10},{8,0},{10,2},{1,5},{3,7},... | collective-permute-start | bytes 1474568 | tf_op jit(solution)/shard_map/ppermute | solution.py:629
  116.8 11.2 %collective-permute-start.20 = (bf16[1,128,384]{2,1,0:T(8,128)(2,1)S(1)}, bf16[1,128,384]{2,1,0:T(8,128)(2,1)S(1)}, u32[]{:S(2)}, u32[]{:S(2)}) collective-permute-start(bf16[1,128,384]{2,1,0:T(8,128)(2,1)S(1)} %get-tuple-element.39), channel_id=1, source_target_pairs={{0,2},{2,0},{4,6},{6,4},{8,10},{10,8},{12,14},{14,12},{1,3},{3,1},... | collective-permute-start | bytes 294920 | tf_op jit(solution)/shard_map/ppermute | solution.py:610
  122.3 21.9 %collective-permute-start.18 = (bf16[1,256,384]{2,1,0:T(8,128)(2,1)S(1)}, bf16[1,256,384]{2,1,0:T(8,128)(2,1)S(1)}, u32[]{:S(2)}, u32[]{:S(2)}) collective-permute-start(bf16[1,256,384]{2,1,0:T(8,128)(2,1)S(1)} %get-tuple-element.37), channel_id=1, source_target_pairs={{0,2},{2,0},{4,6},{6,4},{8,10},{10,8},{12,14},{14,12},{1,3},{3,1},... | collective-permute-start | bytes 589832 | tf_op jit(solution)/shard_map/ppermute | solution.py:610
  139.5 27.3 %collective-permute-start.6 = (bf16[384,640]{1,0:T(8,128)(2,1)S(1)}, bf16[384,640]{1,0:T(8,128)(2,1)S(1)}, u32[]{:S(2)}, u32[]{:S(2)}) collective-permute-start(bf16[384,640]{1,0:T(8,128)(2,1)S(1)} %add_convert_fusion), channel_id=1, source_target_pairs={{0,4},{2,6},{4,12},{6,14},{12,8},{14,10},{8,0},{10,2},{1,5},{3,7},... | collective-permute-start | bytes 1474568 | tf_op jit(solution)/shard_map/ppermute | solution.py:629
